TPU v7x, 512 devices: a whole 4x4x16 slice. The times are simulated.
512 devices in a mesh: dp: 8 (over y, x_hi), context: 64 (over x_lo, z, core).
Axes of the slice: x: 4 (x_hi: 2, x_lo: 2; x = x_hi * 2 + x_lo), y: 4, z: 16, core: 2. Of those that a mesh axis runs over, the one named last changes fastest.
Arguments:
- codes: int32 [8, 65536], P('dp', 'context'), may hold values from 0 to 3
- variant_pos: int32 [8, 64], P('dp'), may hold values from 0 to 65535
- variant_shift: int32 [8, 64], P('dp'), may hold values from 1 to 3
- stem_weight: float32 [15, 4, 384], replicated, may hold values from -1.5 to 1.5
- conv_weight: bfloat16 [5, 384, 384], replicated, may hold values from -0.125 to 0.125
- cotangent: bfloat16 [8, 32768, 384], P('dp', 'context'), may hold values from -6 to 6
Outputs:
- features: bfloat16 [8, 32768, 384], P('dp', 'context')
- d_pooled: bfloat16 [8, 32768, 384], P('dp', 'context')
- conv_grad: float32 [5, 384, 384], replicated
- stem_grad: float32 [15, 4, 384], replicated
All inputs are finite; a program needn't handle non-finite values.
Results may differ from a plain program's by a relative error of at most 0.009.
Values may be sent and summed in bfloat16 or wider, within the bound.
A program may use at most 64 MiB of HBM per device.

v0:
```python
import math

import jax
import jax.numpy as jnp
from jax import lax
from jax.sharding import PartitionSpec as P

root_scale = math.sqrt(2.0 / math.pi)
cubic = 0.044715


def with_halo(block, sides, width):
    for axis, dim in sides:
        count = lax.axis_size(axis)
        forward = [(i, i + 1) for i in range(count - 1)]
        backward = [(target, source) for source, target in forward]
        low = lax.ppermute(
            lax.slice_in_dim(block, block.shape[dim] - width, None, axis=dim), axis, forward
        )
        high = lax.ppermute(lax.slice_in_dim(block, 0, width, axis=dim), axis, backward)
        block = jnp.concatenate([low, block, high], axis=dim)
    return block


def gelu_tanh(value):
    return 0.5 * value * (1.0 + jnp.tanh(root_scale * (value + cubic * value * value * value)))


def gelu_slope(value):
    inner = jnp.tanh(root_scale * (value + cubic * value * value * value))
    return 0.5 * (1.0 + inner) + 0.5 * value * (1.0 - inner * inner) * root_scale * (
        1.0 + 3.0 * cubic * value * value
    )


def per_device(codes, variant_pos, variant_shift, stem_weight, conv_weight, cotangent):
    length = codes.shape[1]
    half_rows = length // 2
    width = stem_weight.shape[2]
    first_base = lax.axis_index("context") * length
    places = first_base + jnp.arange(length, dtype=jnp.int32)
    matches = (variant_pos[:, None, :] == places[None, :, None]).astype(jnp.int32)
    shifts = jnp.sum(matches * variant_shift[:, None, :], axis=2)
    mutated = (codes + shifts) % 4 + 1
    extended = with_halo(mutated, (("context", 1),), 7)
    onehot = (extended[:, :, None] == jnp.arange(1, 5, dtype=jnp.int32)[None, None, :]).astype(
        jnp.float32
    )
    windows = jnp.concatenate([onehot[:, k : k + length] for k in range(15)], axis=2)
    flat_stem = stem_weight.reshape(60, width)
    stem = jnp.einsum(
        "blk,kc->blc",
        windows,
        flat_stem,
        precision=lax.Precision.HIGHEST,
        preferred_element_type=jnp.float32,
    )
    active = gelu_tanh(stem)
    pooled = (0.5 * (active[:, 0::2] + active[:, 1::2])).astype(jnp.bfloat16)
    pooled_f = pooled.astype(jnp.float32)
    gated = gelu_tanh(pooled_f).astype(jnp.bfloat16)
    gated_ext = with_halo(gated, (("context", 1),), 2)
    cot_ext = with_halo(cotangent, (("context", 1),), 2)
    conv_out = jnp.zeros((gated.shape[0], half_rows, width), jnp.float32)
    back = jnp.zeros((gated.shape[0], half_rows, width), jnp.float32)
    for offset in range(5):
        conv_out = conv_out + jnp.einsum(
            "brc,cd->brd",
            gated_ext[:, offset : offset + half_rows],
            conv_weight[offset],
            preferred_element_type=jnp.float32,
        )
        back = back + jnp.einsum(
            "brd,cd->brc",
            cot_ext[:, 4 - offset : 4 - offset + half_rows],
            conv_weight[offset],
            preferred_element_type=jnp.float32,
        )
    features = (pooled_f + conv_out).astype(jnp.bfloat16)
    dpool = cotangent.astype(jnp.float32) + back * gelu_slope(pooled_f)
    d_pooled = dpool.astype(jnp.bfloat16)
    tap_grads = jnp.stack(
        [
            jnp.einsum(
                "brc,brd->cd",
                gated_ext[:, offset : offset + half_rows],
                cotangent,
                preferred_element_type=jnp.float32,
            )
            for offset in range(5)
        ]
    )
    dstem = 0.5 * jnp.repeat(dpool, 2, axis=1) * gelu_slope(stem)
    stem_part = jnp.einsum(
        "blk,blc->kc",
        windows,
        dstem,
        precision=lax.Precision.HIGHEST,
        preferred_element_type=jnp.float32,
    )
    stem_grad = lax.psum(stem_part, ("dp", "context")).reshape(15, 4, width)
    conv_grad = lax.psum(tap_grads, ("dp", "context"))
    return (features, d_pooled, conv_grad, stem_grad)


def solution(mesh):
    placed = (P("dp", "context"), P("dp", None), P("dp", None), P(), P(), P("dp", "context", None))
    return jax.shard_map(
        per_device,
        mesh=mesh,
        in_specs=placed,
        out_specs=(P("dp", "context", None), P("dp", "context", None), P(), P()),
        check_vma=False,
    )
```

profile of v0, /device:TPU:1, one launch (start us, length us, event | category | flops | bytes accessed | tf_op | source)
XLA Modules:
  0.0 565.7 jit_solution(724238133295681119)
XLA Ops:
  7.2 0.0 all-reduce.3.cloned.1.call-start
  7.2 0.8 select_reduce_fusion
  8.0 0.7 fusion.93
  8.7 0.1 fusion.114
  8.8 8.7 %collective-permute-start.1 = (s32[1,7]{1,0:T(1,128)S(1)}, s32[1,7]{1,0:T(1,128)S(1)}, u32[]{:S(2)}, u32[]{:S(2)}) collective-permute-start(s32[1,7]{1,0:T(1,128)S(1)} %get-tuple-element.14), channel_id=1, source_target_pairs={{1,0},{2,1},{3,2},{4,3},{5,4},{6,5},{7,6},{8,7},{9,8},{10,9},{11,1... | collective-permute-start | bytes 92 | tf_op jit(solution)/shard_map/ppermute | solution.py:20
  17.5 1.9 collective-permute-start
  19.5 1.3 fusion.112
  20.7 1.9 collective-permute-start.5
  22.7 2.4 collective-permute-start.4
  25.1 1.8 constant_dynamic-update-slice_fusion.16
  26.9 0.9 reshape.259
  27.8 2.4 fusion.59
  30.2 0.0 collective-permute-done.1
  30.2 0.0 collective-permute-done
  30.2 0.1 concatenate.26
  30.3 0.1 compare_convert_fusion
  30.4 0.1 constant_dynamic-update-slice_fusion.13
  30.5 0.1 constant_dynamic-update-slice_fusion.12
  30.6 0.1 constant_dynamic-update-slice_fusion.11
  30.7 0.1 constant_dynamic-update-slice_fusion.10
  30.8 0.1 constant_dynamic-update-slice_fusion.9
  31.0 0.1 constant_dynamic-update-slice_fusion.8
  31.1 0.1 constant_dynamic-update-slice_fusion.7
  31.2 0.1 constant_dynamic-update-slice_fusion.6
  31.3 0.1 constant_dynamic-update-slice_fusion.5
  31.4 0.1 constant_dynamic-update-slice_fusion.4
  31.5 0.1 constant_dynamic-update-slice_fusion.3
  31.6 0.1 constant_dynamic-update-slice_fusion.2
  31.7 0.1 constant_dynamic-update-slice_fusion.1
  31.8 0.1 constant_dynamic-update-slice_fusion
  31.9 1.4 fusion.75
  33.4 0.5 multiply_bitcast_fusion
  33.9 2.8 slice.143
  36.7 2.8 slice.142
  39.4 1.9 fusion.29
  41.3 0.0 copy-start.6
  41.3 0.6 fusion.113
  42.0 1.9 collective-permute-start.3
  43.9 3.8 collective-permute-start.2
  47.8 0.4 fusion.51
  48.2 0.0 copy-start.2
  48.2 0.4 fusion.18
  48.7 0.5 copy-done.2
  49.2 0.4 convolution_add_fusion.1
  49.6 1.6 multiply_bitcast_fusion.1
  51.2 0.5 broadcast_in_dim.2
  51.8 2.2 mul.172
  54.0 3.6 fusion.6
  57.6 0.7 reshape.270
  58.3 1.2 fusion.25
  59.5 1.2 fusion.24
  60.7 1.3 fusion.23
  62.0 1.2 fusion.22
  63.3 1.2 fusion.21
  64.5 0.0 all-reduce.3.cloned.1.call-update
  64.5 1.3 copy-done.1
  65.9 0.4 fusion.70
  66.3 0.4 convolution_add_fusion.6
  66.7 0.4 convolution_add_fusion.5
  67.1 0.4 convolution_add_fusion.4
  67.5 1.1 fusion.20
  68.7 485.8 %all-reduce.3.cloned.1.call-done = (f32[5,384,384]{2,1,0:T(8,128)}, f32[15,4,384]{2,1,0:T(4,128)}) async-done(((f32[5,384,384]{2,1,0:T(8,128)}, f32[15,4,384]{2,1,0:T(4,128)}), (f32[5,384,384]{2,1,0:T(8,128)}, f32[15,4,384]{2,1,0:T(4,128)})) %all-reduce.3.cloned.1.call-update) | async-done | bytes 3041296 | tf_op jit(solution)/shard_map/psum | solution.py:102
  554.5 3.7 copy.40
  558.2 0.6 copy.41
  (25 shorter events, 0.1 us)
Async XLA Ops:
  7.2 547.3 %all-reduce.3.cloned.1.call-start = ((), (), s32[]{:S(2)}) async-start(), calls=%async_computation | async-start | bytes 6082560 | tf_op jit(solution)/shard_map/psum | solution.py:102
  8.8 21.4 %collective-permute-start.1 = (s32[1,7]{1,0:T(1,128)S(1)}, s32[1,7]{1,0:T(1,128)S(1)}, u32[]{:S(2)}, u32[]{:S(2)}) collective-permute-start(s32[1,7]{1,0:T(1,128)S(1)} %get-tuple-element.14), channel_id=1, source_target_pairs={{1,0},{2,1},{3,2},{4,3},{5,4},{6,5},{7,6},{8,7},{9,8},{10,9},{11,1... | collective-permute-start | bytes 92 | tf_op jit(solution)/shard_map/ppermute | solution.py:20
  17.5 12.7 %collective-permute-start = (s32[1,7]{1,0:T(1,128)S(1)}, s32[1,7]{1,0:T(1,128)S(1)}, u32[]{:S(2)}, u32[]{:S(2)}) collective-permute-start(s32[1,7]{1,0:T(1,128)S(1)} %get-tuple-element.15), channel_id=1, source_target_pairs={{0,1},{1,2},{2,3},{3,4},{4,5},{5,6},{6,7},{7,8},{8,9},{9,10},{10,1... | collective-permute-start | bytes 92 | tf_op jit(solution)/shard_map/ppermute | solution.py:17
  20.7 27.9 %collective-permute-start.5 = (bf16[1,2,384]{2,1,0:T(2,128)(2,1)}, bf16[1,2,384]{2,1,0:T(2,128)(2,1)S(1)}, u32[]{:S(2)}, u32[]{:S(2)}) collective-permute-start(bf16[1,2,384]{2,1,0:T(2,128)(2,1)} %get-tuple-element.10), channel_id=1, source_target_pairs={{0,1},{1,2},{2,3},{3,4},{4,5},{5,6},{6,7},{7,8},{8,9},{9,10},{10,1... | collective-permute-start | bytes 4616 | tf_op jit(solution)/shard_map/ppermute | solution.py:17
  22.7 25.1 %collective-permute-start.4 = (bf16[1,2,384]{2,1,0:T(2,128)(2,1)}, bf16[1,2,384]{2,1,0:T(2,128)(2,1)S(1)}, u32[]{:S(2)}, u32[]{:S(2)}) collective-permute-start(bf16[1,2,384]{2,1,0:T(2,128)(2,1)} %get-tuple-element.11), channel_id=1, source_target_pairs={{1,0},{2,1},{3,2},{4,3},{5,4},{6,5},{7,6},{8,7},{9,8},{10,9},{11,1... | collective-permute-start | bytes 4616 | tf_op jit(solution)/shard_map/ppermute | solution.py:20
  31.9 1.9 copy-start.8
  39.4 8.3 %copy-start.4 = (bf16[1,514,384]{2,1,0:T(8,128)(2,1)S(1)}, bf16[1,514,384]{2,1,0:T(8,128)(2,1)}, u32[]{:S(2)}) copy-start(bf16[1,514,384]{2,1,0:T(8,128)(2,1)} %constant_dynamic-update-slice_fusion.16) | copy-start | bytes 1184260
  39.4 8.3 %copy-start = (bf16[5,384,384]{2,1,0:T(8,128)(2,1)S(1)}, bf16[5,384,384]{2,1,0:T(8,128)(2,1)}, u32[]{:S(2)}) copy-start(bf16[5,384,384]{2,1,0:T(8,128)(2,1)} %param.10) | copy-start | bytes 4423684
  39.4 8.7 %copy-start.5 = (f32[512,384]{1,0:T(8,128)S(1)}, f32[512,384]{1,0:T(8,128)}, u32[]{:S(2)}) copy-start(f32[512,384]{1,0:T(8,128)} %fusion.59) | copy-start | bytes 2359300
  41.3 8.3 %copy-start.6 = (bf16[1,512,384]{2,1,0:T(8,128)(2,1)}, bf16[1,512,384]{2,1,0:T(8,128)(2,1)S(1)}, u32[]{:S(2)}) copy-start(bf16[1,512,384]{2,1,0:T(8,128)(2,1)S(1)} %get-tuple-element.7) | copy-start | bytes 1179652
  42.0 20.1 %collective-permute-start.3 = (bf16[1,2,384]{2,1,0:T(2,128)(2,1)}, bf16[1,2,384]{2,1,0:T(2,128)(2,1)S(1)}, u32[]{:S(2)}, u32[]{:S(2)}) collective-permute-start(bf16[1,2,384]{2,1,0:T(2,128)(2,1)} %get-tuple-element.12), channel_id=1, source_target_pairs={{1,0},{2,1},{3,2},{4,3},{5,4},{6,5},{7,6},{8,7},{9,8},{10,9},{11,1... | collective-permute-start | bytes 4616 | tf_op jit(solution)/shard_map/ppermute | solution.py:20
  43.9 14.4 %collective-permute-start.2 = (bf16[1,2,384]{2,1,0:T(2,128)(2,1)}, bf16[1,2,384]{2,1,0:T(2,128)(2,1)S(1)}, u32[]{:S(2)}, u32[]{:S(2)}) collective-permute-start(bf16[1,2,384]{2,1,0:T(2,128)(2,1)} %get-tuple-element.13), channel_id=1, source_target_pairs={{0,1},{1,2},{2,3},{3,4},{4,5},{5,6},{6,7},{7,8},{8,9},{9,10},{10,1... | collective-permute-start | bytes 4616 | tf_op jit(solution)/shard_map/ppermute | solution.py:17
  48.2 1.0 copy-start.2
  54.0 4.3 copy-start.3
  58.2 2.5 copy-start.7
  64.5 1.4 copy-start.1
  554.5 3.7 copy-start.9
Sparse Core Ops, SparseCore 0:
  64.6 489.8 all-reduce.2
where the time goes:
time: 568 us; the launch traced here: 566 us
  waiting for transfers between devices  486 us (86%)
  local copies, waits for them, and re-layouts  21.4 us (4%)
  starting transfers between devices  20.7 us (4%)
  matrix products  19.3 us (3%)
  between operations  14.4 us (3%)
    psum x1, waiting for transfers between devices, per_device(): conv_grad = lax.psum(tap_grads, ('dp', 'context'))  486 us
    ppermute x3, starting transfers between devices, with_halo(): lax.ppermute(lax.slice_in_dim(block, 0, width, axis=dim), axis, backward)  13 us
  transfers between devices with their start and end apart: 7, of which 1 were waited for; matrix products, arithmetic and copies ran while one was open for 6% of the time, Pallas kernels for 0%

commit v1 on v0

--- a/solution.py
+++ b/solution.py
@@ -1,12 +1,299 @@
 import math
+import functools
 
 import jax
 import jax.numpy as jnp
 from jax import lax
+from jax.experimental import pallas as pl
+from jax.experimental.pallas import tpu as pltpu
+
+MESH = pl.DeviceIdType.MESH
+SUB = 96
 from jax.sharding import PartitionSpec as P
+
 
 root_scale = math.sqrt(2.0 / math.pi)
 cubic = 0.044715
+
+
+def places(ring, deep, high):
+    low = ring // high
+    dp, ctx = lax.axis_index("dp"), lax.axis_index("context")
+    y, xh = lax.div(dp, high), lax.rem(dp, high)
+    core, z = lax.rem(ctx, 2), lax.rem(lax.div(ctx, 2), deep)
+    x = xh * low + lax.div(ctx, 2 * deep)
+
+    def device(x, y, z, core):
+        return {
+            "dp": y * high + lax.div(x, low),
+            "context": (lax.rem(x, low) * deep + z) * 2 + core,
+        }
+
+    return x, y, z, core, device
+
+
+def reduce_kernel(
+    ring, deep, high, part, gathered,
+    s0, r0, s1, r1, a2, s2, r2, v3, s3, r3, g3, w3,
+    c0s, c0r, c1s, c1r, c2s, c2r, c3s, c3r, d3s, d3r, d2s, d2r, d1s, d1r, d0s, d0r,
+):
+    f32, bf16 = jnp.float32, jnp.bfloat16
+    x, y, z, core, device = places(ring, deep, high)
+    other = 1 - core
+    per = 16 // ring
+    fine = per // ring
+
+    def along(half, level, step):
+        if (half == 0) == (level == 1):
+            return device(lax.rem(x + step, ring), y, z, core)
+        return device(x, lax.rem(y + step, ring), z, core)
+
+    def mine(half, level):
+        return x if (half == 0) == (level == 1) else y
+
+    def deeper(step):
+        return device(x, y, lax.rem(z + step, deep), core)
+
+    sibling = device(x, y, z, other)
+
+    barrier = pltpu.get_barrier_semaphore()
+    pl.semaphore_signal(barrier, inc=1, device_id=sibling, device_id_type=MESH)
+    for step in range(1, ring):
+        for half in range(2):
+            pl.semaphore_signal(barrier, inc=1, device_id=along(half, 1, step), device_id_type=MESH)
+
+    def greet(step, carry):
+        pl.semaphore_signal(barrier, inc=1, device_id=deeper(step), device_id_type=MESH)
+        return carry
+
+    lax.fori_loop(1, deep, greet, 0)
+    pl.semaphore_wait(barrier, 1 + 2 * (ring - 1) + deep - 1)
+
+    def remote(src, dst, send, recv, to):
+        return pltpu.make_async_remote_copy(
+            src_ref=src, dst_ref=dst, send_sem=send, recv_sem=recv, device_id=to, device_id_type=MESH
+        )
+
+    order = sorted(range(1, ring), key=lambda d: -min(d, ring - d)) + [0]
+
+    def level0(half, step):
+        piece = lax.rem(mine(half, 1) + step, ring)
+        return remote(
+            s0.at[half, piece], r0.at[half, piece], c0s.at[half, step], c0r.at[half, step], sibling
+        )
+
+    for step in order:
+        for half in range(2):
+            piece = lax.rem(mine(half, 1) + step, ring)
+            s0[half, piece] = part[other, half, piece].astype(bf16)
+            level0(half, step).start()
+
+    def level1(half, step):
+        piece = lax.rem(mine(half, 1) + step, ring)
+        return remote(
+            s1.at[half, step - 1], r1.at[half, step - 1], c1s.at[half, step - 1], c1r.at[half, step - 1],
+            along(half, 1, step),
+        )
+
+    for step in order:
+        for half in range(2):
+            piece = lax.rem(mine(half, 1) + step, ring)
+            level0(half, step).wait_recv()
+            if step:
+                s1[half, step - 1] = (part[core, half, piece] + r0[half, piece].astype(f32)).astype(bf16)
+                level1(half, step).start()
+
+    def level2(half, step):
+        return remote(
+            s2.at[half, lax.rem(mine(half, 2) + step, ring)], r2.at[half, step - 1],
+            c2s.at[half, step - 1], c2r.at[half, step - 1], along(half, 2, step),
+        )
+
+    for half in range(2):
+        piece = mine(half, 1)
+        total = part[core, half, piece] + r0[half, piece].astype(f32)
+        for step in range(1, ring):
+            level1(half, step).wait_recv()
+            total = total + r1[half, step - 1].astype(f32)
+        total = total.reshape(a2.shape[1:])
+        a2[half] = total
+        s2[half] = total.astype(bf16)
+        for step in order[:-1]:
+            level2(half, step).start()
+
+    rows = fine * SUB
+    for half in range(2):
+        total = a2[half, mine(half, 2)]
+        for step in range(1, ring):
+            level2(half, step).wait_recv()
+            total = total + r2[half, step - 1].astype(f32)
+        v3[half * rows : (half + 1) * rows] = total
+    share = 2 * rows // deep
+    wide = s3.shape[1]
+    for piece in range(deep):
+        s3[piece] = v3[piece * share : piece * share + wide].astype(bf16)
+
+    def level3(step):
+        return remote(
+            s3.at[lax.rem(z + step, deep)], r3.at[step - 1], c3s.at[step - 1], c3r.at[step - 1], deeper(step)
+        )
+
+    def back3(step):
+        return remote(g3.at[z], g3.at[z], d3s.at[step - 1], d3r.at[step - 1], deeper(step))
+
+    def far(i):
+        near = deep // 2 - lax.div(i + 1, 2)
+        return jnp.where(lax.rem(i, 2) == 0, near, deep - near)
+
+    def send3(i, carry):
+        level3(far(i)).start()
+        return carry
+
+    lax.fori_loop(0, deep - 1, send3, 0)
+
+    def take3(i, total):
+        step = i + 1
+        level3(step).wait_recv()
+        return total + r3[i].astype(f32)
+
+    total = lax.fori_loop(0, deep - 1, take3, s3[z].astype(f32))
+    g3[z] = total.astype(bf16)
+
+    def spread3(i, carry):
+        back3(far(i)).start()
+        return carry
+
+    lax.fori_loop(0, deep - 1, spread3, 0)
+
+    def got3(i, carry):
+        back3(i + 1).wait_recv()
+        return carry
+
+    lax.fori_loop(0, deep - 1, got3, 0)
+    for piece in range(deep):
+        w3[piece * share : piece * share + wide] = g3[piece].astype(f32)
+
+    def back2(half, step):
+        spot = gathered.at[core, half, mine(half, 1), mine(half, 2)]
+        return remote(spot, spot, d2s.at[half, step - 1], d2r.at[half, step - 1], along(half, 2, step))
+
+    for half in range(2):
+        gathered[core, half, mine(half, 1), mine(half, 2)] = w3[half * rows : (half + 1) * rows].astype(bf16)
+        for step in order[:-1]:
+            back2(half, step).start()
+
+    def back1(half, step):
+        spot = gathered.at[core, half, mine(half, 1)]
+        return remote(spot, spot, d1s.at[half, step - 1], d1r.at[half, step - 1], along(half, 1, step))
+
+    def back0(half, step):
+        spot = gathered.at[core, half, lax.rem(mine(half, 1) + ring - step, ring)]
+        return remote(spot, spot, d0s.at[half, step], d0r.at[half, step], sibling)
+
+    for half in range(2):
+        for step in range(1, ring):
+            back2(half, step).wait_recv()
+        for step in order[:-1]:
+            back1(half, step).start()
+        back0(half, 0).start()
+    near = sorted(range(1, ring), key=lambda d: min(d, ring - d))
+    for step in near:
+        for half in range(2):
+            back1(half, step).wait_recv()
+            back0(half, step).start()
+    for half in range(2):
+        for step in range(ring):
+            back0(half, step).wait()
+            level0(half, step).wait_send()
+        for step in range(1, ring):
+            level1(half, step).wait_send()
+            level2(half, step).wait_send()
+            back2(half, step).wait_send()
+            back1(half, step).wait_send()
+
+    def sent3(i, carry):
+        level3(i + 1).wait_send()
+        back3(i + 1).wait_send()
+        return carry
+
+    lax.fori_loop(0, deep - 1, sent3, 0)
+
+
+def all_reduce(ring, deep, high, part):
+    f32, bf16 = jnp.float32, jnp.bfloat16
+    per = 16 // ring
+    fine = per // ring
+    share = 2 * fine * SUB // deep
+    wide = -(-share // 16) * 16
+    dma = pltpu.SemaphoreType.DMA
+    level = lambda *lead: pltpu.VMEM((2,) + lead, bf16)
+    pair = lambda *dims: [dma(dims), dma(dims)]
+    return pl.pallas_call(
+        functools.partial(reduce_kernel, ring, deep, high),
+        out_shape=jax.ShapeDtypeStruct((2, 2, ring, ring, fine * SUB, 128), bf16),
+        in_specs=[pl.BlockSpec(memory_space=pltpu.VMEM)],
+        out_specs=pl.BlockSpec(memory_space=pltpu.VMEM),
+        scratch_shapes=[
+            level(ring, per * SUB, 128),
+            level(ring, per * SUB, 128),
+            level(ring - 1, per * SUB, 128),
+            level(ring - 1, per * SUB, 128),
+            pltpu.VMEM((2, ring, fine * SUB, 128), f32),
+            level(ring, fine * SUB, 128),
+            level(ring - 1, fine * SUB, 128),
+            pltpu.VMEM((2 * fine * SUB + wide, 128), f32),
+            pltpu.VMEM((deep, wide, 128), bf16),
+            pltpu.VMEM((deep - 1, wide, 128), bf16),
+            pltpu.VMEM((deep, wide, 128), bf16),
+            pltpu.VMEM((2 * fine * SUB + wide, 128), f32),
+            *pair(2, ring), *pair(2, ring - 1), *pair(2, ring - 1), *pair(deep - 1),
+            *pair(deep - 1), *pair(2, ring - 1), *pair(2, ring - 1), *pair(2, ring),
+        ],
+        compiler_params=pltpu.CompilerParams(collective_id=0, has_side_effects=True),
+        name="reduce",
+    )(part.reshape(2, 2, ring, per * SUB, 128))
+
+
+def finish_kernel(summed, conv, stem):
+    t = pl.program_id(0)
+    for k in range(3):
+        for r in range(4):
+            n = 12 * t + 4 * k + r
+            conv[0, r * SUB : (r + 1) * SUB, k * 128 : (k + 1) * 128] = summed[
+                lax.div(n, 15), lax.rem(n, 15)
+            ].astype(jnp.float32)
+
+    @pl.when(t == 0)
+    def _():
+        rows = jnp.concatenate([summed[0, 15], summed[2, 15]], axis=0).astype(jnp.float32)
+        for k in range(3):
+            for tap in range(15):
+                stem[tap, :, k * 128 : (k + 1) * 128] = rows[k * 64 + 4 * tap : k * 64 + 4 * tap + 4]
+
+
+def finish(summed):
+    return pl.pallas_call(
+        finish_kernel,
+        grid=(5,),
+        out_shape=(
+            jax.ShapeDtypeStruct((5, 384, 384), jnp.float32),
+            jax.ShapeDtypeStruct((15, 4, 384), jnp.float32),
+        ),
+        in_specs=[pl.BlockSpec((4, 16, SUB, 128), lambda t: (0, 0, 0, 0))],
+        out_specs=(
+            pl.BlockSpec((1, 384, 384), lambda t: (t, 0, 0)),
+            pl.BlockSpec((15, 4, 384), lambda t: (0, 0, 0)),
+        ),
+        name="finish",
+    )(summed.reshape(4, 16, SUB, 128))
+
+
+def pack(taps, stem):
+    width = 384
+    blocks = taps.reshape(5, 4, SUB, 3, 128).transpose(0, 3, 1, 2, 4).reshape(4, 15, SUB, 128)
+    stem = jnp.pad(stem, ((0, 4), (0, 0))).reshape(64, 3, 128).transpose(1, 0, 2).reshape(2, SUB, 128)
+    last = jnp.zeros((4, 1, SUB, 128), jnp.float32).at[0, 0].set(stem[0]).at[2, 0].set(stem[1])
+    return jnp.concatenate([blocks, last], axis=1).reshape(2, 2, 16 * SUB, 128)
 
 
 def with_halo(block, sides, width):
@@ -98,8 +385,7 @@
         precision=lax.Precision.HIGHEST,
         preferred_element_type=jnp.float32,
     )
-    stem_grad = lax.psum(stem_part, ("dp", "context")).reshape(15, 4, width)
-    conv_grad = lax.psum(tap_grads, ("dp", "context"))
+    conv_grad, stem_grad = finish(all_reduce(4, 16, 2, pack(tap_grads, stem_part[0] if stem_part.ndim == 3 else stem_part)))
     return (features, d_pooled, conv_grad, stem_grad)
 
 

time: 568 us -> 130 us (0.23)
  waiting for transfers between devices: 486 us -> 0.02 us
  Pallas kernels: 0 us -> 59.6 us
  between operations: 14.4 us -> 1.2 us
    psum x1 -> x0, waiting for transfers between devices: 486 us -> none  [per_device(): conv_grad = lax.psum(tap_grads, ('dp', 'context'))]
    pallas_call x0 -> x2, Pallas kernels: none -> 59.6 us  [the longest x1 55.5 us: all_reduce(): pl.pallas_call(functools.partial(reduce_kernel, ring, deep, high), out_sh...]
    dot_general x0 -> x5, local copies, waits for them, and re-layouts: none -> 7.65 us  [per_device(): jnp.einsum('brc,brd->cd', gated_ext[:, offset:offset + half_rows], cotang...]
  transfers between devices with their start and end apart: 7 -> 6, of which waited for: 1 -> 0; matrix products, arithmetic and copies ran while one was open for 6% -> 22% of each run, Pallas kernels for 0% -> 0%
where the time goes in v1:
time: 130 us; the launch traced here: 129 us
  Pallas kernels  59.6 us (46%)
  local copies, waits for them, and re-layouts  24.3 us (19%)
  starting transfers between devices  20.7 us (16%)
  matrix products  16.3 us (13%)
  other arithmetic  7.03 us (5%)
    pallas_call x1, Pallas kernels, all_reduce(): pl.pallas_call(functools.partial(reduce_kernel, ring, deep, high), out_sh...  55.5 us
    ppermute x3, starting transfers between devices, with_halo(): lax.ppermute(lax.slice_in_dim(block, 0, width, axis=dim), axis, backward)  13.1 us
    dot_general x5, local copies, waits for them, and re-layouts, per_device(): jnp.einsum('brc,brd->cd', gated_ext[:, offset:offset + half_rows], cotang...  7.65 us
    ppermute x3, starting transfers between devices, with_halo(): lax.ppermute(lax.slice_in_dim(block, block.shape[dim] - width, None, axis...  7.65 us
    unnamed x48, local copies, waits for them, and re-layouts  6.91 us
    slice x2, local copies, waits for them, and re-layouts, per_device(): pooled = (0.5 * (active[:, 0::2] + active[:, 1::2])).astype(jnp.bfloat16)  5.56 us
    dot_general x5, matrix products, per_device(): jnp.einsum('brd,cd->brc', cot_ext[:, 4 - offset:4 - offset + half_rows],...  5.11 us
    pallas_call x1, Pallas kernels, finish(): pl.pallas_call(finish_kernel, grid=(5,), out_shape=(jax.ShapeDtypeStruct(...  4.06 us
  transfers between devices with their start and end apart: 6, of which 0 were waited for; matrix products, arithmetic and copies ran while one was open for 22% of the time, Pallas kernels for 0%

profile of v1, /device:TPU:1, one launch (start us, length us, event | category | flops | bytes accessed | tf_op | source)
XLA Modules:
  0.0 129.1 jit_solution(12732653280332205344)
XLA Ops:
  0.7 0.8 select_reduce_fusion
  1.5 0.7 fusion.86
  2.3 8.7 %collective-permute-start.1 = (s32[1,7]{1,0:T(1,128)S(1)}, s32[1,7]{1,0:T(1,128)S(1)}, u32[]{:S(2)}, u32[]{:S(2)}) collective-permute-start(s32[1,7]{1,0:T(1,128)S(1)} %get-tuple-element.46), channel_id=1, source_target_pairs={{1,0},{2,1},{3,2},{4,3},{5,4},{6,5},{7,6},{8,7},{9,8},{10,9},{11,1... | collective-permute-start | bytes 92 | tf_op jit(solution)/shard_map/ppermute | solution.py:307
  11.0 1.9 %collective-permute-start = (s32[1,7]{1,0:T(1,128)S(1)}, s32[1,7]{1,0:T(1,128)S(1)}, u32[]{:S(2)}, u32[]{:S(2)}) collective-permute-start(s32[1,7]{1,0:T(1,128)S(1)} %get-tuple-element.47), channel_id=1, source_target_pairs={{0,1},{1,2},{2,3},{3,4},{4,5},{5,6},{6,7},{7,8},{8,9},{9,10},{10,1... | collective-permute-start | bytes 92 | tf_op jit(solution)/shard_map/ppermute | solution.py:304
  13.0 0.7 fusion.101
  13.7 1.9 %collective-permute-start.5 = (bf16[1,2,384]{2,1,0:T(2,128)(2,1)S(1)}, bf16[1,2,384]{2,1,0:T(2,128)(2,1)S(1)}, u32[]{:S(2)}, u32[]{:S(2)}) collective-permute-start(bf16[1,2,384]{2,1,0:T(2,128)(2,1)S(1)} %get-tuple-element.42), channel_id=1, source_target_pairs={{0,1},{1,2},{2,3},{3,4},{4,5},{5,6},{6,7},{7,8},{8,9},{9,10},{10,1... | collective-permute-start | bytes 4616 | tf_op jit(solution)/shard_map/ppermute | solution.py:304
  15.6 2.4 %collective-permute-start.4 = (bf16[1,2,384]{2,1,0:T(2,128)(2,1)S(1)}, bf16[1,2,384]{2,1,0:T(2,128)(2,1)S(1)}, u32[]{:S(2)}, u32[]{:S(2)}) collective-permute-start(bf16[1,2,384]{2,1,0:T(2,128)(2,1)S(1)} %get-tuple-element.43), channel_id=1, source_target_pairs={{1,0},{2,1},{3,2},{4,3},{5,4},{6,5},{7,6},{8,7},{9,8},{10,9},{11,1... | collective-permute-start | bytes 4616 | tf_op jit(solution)/shard_map/ppermute | solution.py:307
  18.0 1.2 copy.37
  19.2 1.0 constant_dynamic-update-slice_fusion.16
  20.3 2.3 %fusion.50 = f32[512,384]{1,0:T(8,128)} fusion(bf16[1,512,384]{2,1,0:T(8,128)(2,1)S(1)} %copy-done, bf16[5,384,384]{2,1,0:T(8,128)(2,1)} %param.14), kind=kOutput, calls=%fused_computation.83 | convolution fusion | flops 150994944 | bytes 1474560 | tf_op jit(solution)/shard_map/brd,cd->brc/dot_general | solution.py:360
  22.6 0.1 concatenate.35
  22.8 0.1 constant_dynamic-update-slice_fusion.13
  22.9 0.1 constant_dynamic-update-slice_fusion.12
  23.0 0.1 constant_dynamic-update-slice_fusion.11
  23.1 0.1 constant_dynamic-update-slice_fusion.10
  23.2 0.1 constant_dynamic-update-slice_fusion.9
  23.3 0.1 constant_dynamic-update-slice_fusion.8
  23.4 0.1 constant_dynamic-update-slice_fusion.7
  23.6 0.1 constant_dynamic-update-slice_fusion.6
  23.7 0.1 constant_dynamic-update-slice_fusion.5
  23.8 0.1 constant_dynamic-update-slice_fusion.4
  23.9 0.1 constant_dynamic-update-slice_fusion.3
  24.0 0.1 constant_dynamic-update-slice_fusion.2
  24.1 0.1 constant_dynamic-update-slice_fusion.1
  24.2 0.1 constant_dynamic-update-slice_fusion
  24.3 1.5 %fusion.69 = f32[1024,384]{1,0:T(8,128)S(1)} fusion(f32[60,384]{1,0:T(8,128)S(1)} %reshape.396, f32[1,1024,60]{1,0,2:T(1,128)S(1)} %constant_dynamic-update-slice_fusion), kind=kOutput, calls=%fused_computation.102 | convolution fusion | flops 283115520 | bytes 1910784 | tf_op jit(solution)/shard_map/blk,kc->blc/dot_general | solution.py:338
  25.8 1.2 copy-done.1
  27.0 0.5 multiply_bitcast_fusion
  27.4 2.8 %slice.204 = f32[1,512,384]{2,1,0:T(8,128)} slice(f32[1,1024,384]{2,1,0:T(8,128)S(1)} %multiply_bitcast_fusion), slice={[0:1:1], [1:1024:2], [0:384:1]} | slice | bytes 1572864 | tf_op jit(solution)/shard_map/slice | solution.py:346
  30.2 2.8 %slice.203 = f32[1,512,384]{2,1,0:T(8,128)} slice(f32[1,1024,384]{2,1,0:T(8,128)S(1)} %multiply_bitcast_fusion), slice={[0:1:1], [0:1024:2], [0:384:1]} | slice | bytes 1572864 | tf_op jit(solution)/shard_map/slice | solution.py:346
  33.0 1.8 %fusion.29 = (bf16[1,512,384]{2,1,0:T(8,128)(2,1)S(1)}, bf16[1,512,384]{2,1,0:T(8,128)(2,1)S(1)}) fusion(f32[1,512,384]{2,1,0:T(8,128)} %slice.203, f32[1,512,384]{2,1,0:T(8,128)} %slice.204), kind=kLoop, calls=%fused_computation.51 | loop fusion | flops 2555904 | bytes 2359296 | tf_op jit(solution)/shard_map/convert_element_type | solution.py:348
  34.9 1.9 %collective-permute-start.3 = (bf16[1,2,384]{2,1,0:T(2,128)(2,1)S(1)}, bf16[1,2,384]{2,1,0:T(2,128)(2,1)S(1)}, u32[]{:S(2)}, u32[]{:S(2)}) collective-permute-start(bf16[1,2,384]{2,1,0:T(2,128)(2,1)S(1)} %get-tuple-element.44), channel_id=1, source_target_pairs={{1,0},{2,1},{3,2},{4,3},{5,4},{6,5},{7,6},{8,7},{9,8},{10,9},{11,1... | collective-permute-start | bytes 4616 | tf_op jit(solution)/shard_map/ppermute | solution.py:307
  36.8 3.8 %collective-permute-start.2 = (bf16[1,2,384]{2,1,0:T(2,128)(2,1)S(1)}, bf16[1,2,384]{2,1,0:T(2,128)(2,1)S(1)}, u32[]{:S(2)}, u32[]{:S(2)}) collective-permute-start(bf16[1,2,384]{2,1,0:T(2,128)(2,1)S(1)} %get-tuple-element.45), channel_id=1, source_target_pairs={{0,1},{1,2},{2,3},{3,4},{4,5},{5,6},{6,7},{7,8},{8,9},{9,10},{10,1... | collective-permute-start | bytes 4616 | tf_op jit(solution)/shard_map/ppermute | solution.py:304
  40.6 0.9 copy.40
  41.6 0.4 fusion.49
  42.0 0.7 copy-done.4
  42.7 0.4 fusion.18
  43.1 0.4 convolution_add_fusion.1
  43.6 1.6 %multiply_bitcast_fusion.1 = (f32[512,384]{1,0:T(8,128)S(1)}, bf16[1,512,384]{2,1,0:T(8,128)(2,1)}) fusion(bf16[1,512,384]{2,1,0:T(8,128)(2,1)S(1)} %get-tuple-element.33, f32[512,384]{1,0:T(8,128)S(1)} %convolution_add_fusion.1, bf16[5,384,384]{2,1,0:T(8,128)(2,1)S(1)} %copy-done.2, bf16[1,512,384]{2,1,0:T(8,128)(2,1)S(1)} %copy-done, ...), kind=kOutput, calls=%fused_computation.59 | convolution fusion | flops 156499968 | bytes 3442176 | tf_op jit(solution)/shard_map/brd,cd->brc/dot_general | solution.py:360
  45.2 0.5 broadcast_in_dim.2
  45.7 2.2 %mul.172 = f32[1024,384]{1,0:T(8,128)} reshape(f32[512,2,384]{2,1,0:T(2,128)S(1)} %broadcast_in_dim.2) | data formatting | bytes 3145728 | tf_op jit(solution)/shard_map/mul | solution.py:380
  48.0 4.0 %fusion.6 = f32[60,384]{1,0:T(8,128)S(1)} fusion(f32[1024,384]{1,0:T(8,128)} %mul.172, f32[1024,384]{1,0:T(8,128)} %copy-done.1, f32[1,1024,60]{1,0,2:T(1,128)S(1)} %copy-done.14), kind=kOutput, calls=%fused_computation.17 | convolution fusion | flops 290193408 | bytes 3483648 | tf_op jit(solution)/shard_map/blk,blc->kc/dot_general | solution.py:381
  52.1 0.4 fusion.55
  52.5 0.4 convolution_add_fusion.6
  52.9 0.4 convolution_add_fusion.5
  53.3 1.2 fusion.84
  54.6 1.9 %copy.42 = bf16[384,512]{1,0:T(8,128)(2,1)} copy(bf16[384,512]{0,1:T(8,128)(2,1)} %get-tuple-element.36) | data formatting | bytes 786432 | tf_op jit(solution)/shard_map/brc,brd->cd/dot_general | solution.py:371
  56.5 1.9 %copy.41 = bf16[384,512]{1,0:T(8,128)(2,1)} copy(bf16[384,512]{0,1:T(8,128)(2,1)} %get-tuple-element.37) | data formatting | bytes 786432 | tf_op jit(solution)/shard_map/brc,brd->cd/dot_general | solution.py:371
  58.4 1.9 %copy.38 = bf16[384,512]{1,0:T(8,128)(2,1)} copy(bf16[384,512]{0,1:T(8,128)(2,1)} %get-tuple-element.40) | data formatting | bytes 786432 | tf_op jit(solution)/shard_map/brc,brd->cd/dot_general | solution.py:371
  60.3 1.0 copy.39
  61.3 1.4 %fusion.25 = f32[5,4,96,3,128]{4,2,3,1,0:T(8,128)S(1)} fusion(bf16[4,96,512,1]{2,1,3,0:T(8,128)(2,1)} %bitcast.187, bf16[3,128,512,1]{2,1,0,3:T(8,128)(2,1)S(1)} %bitcast.175), kind=kOutput, calls=%fused_computation.48 | convolution fusion | flops 150994944 | bytes 1376256 | tf_op jit(solution)/shard_map/brc,brd->cd/dot_general | solution.py:371
  62.8 0.4 fusion.24
  63.2 0.4 fusion.23
  63.6 0.2 copy-done.9
  63.7 0.4 fusion.22
  64.2 0.4 fusion.21
  64.6 0.3 copy.43
  64.8 0.7 copy-done.12
  65.5 1.8 %pad_maximum_fusion = f32[4,16,96,128]{3,2,1,0:T(8,128)} fusion(f32[4,1,96,128]{3,2,1,0:T(8,128)S(1)} %copy-done.12, f32[4,15,96,128]{3,2,1,0:T(8,128)S(1)} %bitcast.181), kind=kLoop, calls=%fused_computation | loop fusion | flops 786432 | bytes 6291456 | tf_op jit(solution)/shard_map/concatenate | solution.py:296
  67.3 55.5 %reduce.7 = bf16[2,2,4,4,96,128]{5,4,3,2,1,0:T(8,128)(2,1)} custom-call(f32[2,2,4,384,128]{4,3,2,1,0:T(8,128)} %bitcast.180), custom_call_target="tpu_custom_call" | custom-call | tf_op jit(solution)/shard_map/reduce/pallas_call | solution.py:231
  122.9 4.1 %finish.1 = (f32[5,384,384]{2,1,0:T(8,128)}, f32[15,4,384]{2,1,0:T(4,128)}) custom-call(bf16[4,16,96,128]{3,2,1,0:T(8,128)(2,1)} %bitcast.182), custom_call_target="tpu_custom_call" | custom-call | tf_op jit(solution)/shard_map/finish/pallas_call | solution.py:275
  127.0 0.4 convolution_add_fusion.4
  127.4 0.6 copy-done.6
  128.0 1.1 fusion.20
  (48 shorter events, 0.4 us)
Async XLA Ops:
  0.6 19.7 %copy-start = (bf16[1,512,384]{2,1,0:T(8,128)(2,1)S(1)}, bf16[1,512,384]{2,1,0:T(8,128)(2,1)}, u32[]{:S(2)}) copy-start(bf16[1,512,384]{2,1,0:T(8,128)(2,1)} %param.15) | copy-start | bytes 1179652
  0.6 19.6 %copy-start.15 = (f32[15,4,384]{2,1,0:T(4,128)S(1)}, f32[15,4,384]{2,1,0:T(4,128)}, u32[]{:S(2)}) copy-start(f32[15,4,384]{2,1,0:T(4,128)} %param.13) | copy-start | bytes 276484
  2.3 20.3 %collective-permute-start.1 = (s32[1,7]{1,0:T(1,128)S(1)}, s32[1,7]{1,0:T(1,128)S(1)}, u32[]{:S(2)}, u32[]{:S(2)}) collective-permute-start(s32[1,7]{1,0:T(1,128)S(1)} %get-tuple-element.46), channel_id=1, source_target_pairs={{1,0},{2,1},{3,2},{4,3},{5,4},{6,5},{7,6},{8,7},{9,8},{10,9},{11,1... | collective-permute-start | bytes 92 | tf_op jit(solution)/shard_map/ppermute | solution.py:307
  11.0 11.5 %collective-permute-start = (s32[1,7]{1,0:T(1,128)S(1)}, s32[1,7]{1,0:T(1,128)S(1)}, u32[]{:S(2)}, u32[]{:S(2)}) collective-permute-start(s32[1,7]{1,0:T(1,128)S(1)} %get-tuple-element.47), channel_id=1, source_target_pairs={{0,1},{1,2},{2,3},{3,4},{4,5},{5,6},{6,7},{7,8},{8,9},{9,10},{10,1... | collective-permute-start | bytes 92 | tf_op jit(solution)/shard_map/ppermute | solution.py:304
  13.7 29.4 %collective-permute-start.5 = (bf16[1,2,384]{2,1,0:T(2,128)(2,1)S(1)}, bf16[1,2,384]{2,1,0:T(2,128)(2,1)S(1)}, u32[]{:S(2)}, u32[]{:S(2)}) collective-permute-start(bf16[1,2,384]{2,1,0:T(2,128)(2,1)S(1)} %get-tuple-element.42), channel_id=1, source_target_pairs={{0,1},{1,2},{2,3},{3,4},{4,5},{5,6},{6,7},{7,8},{8,9},{9,10},{10,1... | collective-permute-start | bytes 4616 | tf_op jit(solution)/shard_map/ppermute | solution.py:304
  15.6 26.0 %collective-permute-start.4 = (bf16[1,2,384]{2,1,0:T(2,128)(2,1)S(1)}, bf16[1,2,384]{2,1,0:T(2,128)(2,1)S(1)}, u32[]{:S(2)}, u32[]{:S(2)}) collective-permute-start(bf16[1,2,384]{2,1,0:T(2,128)(2,1)S(1)} %get-tuple-element.43), channel_id=1, source_target_pairs={{1,0},{2,1},{3,2},{4,3},{5,4},{6,5},{7,6},{8,7},{9,8},{10,9},{11,1... | collective-permute-start | bytes 4616 | tf_op jit(solution)/shard_map/ppermute | solution.py:307
  24.3 3.1 %copy-start.13 = (f32[1,1024,60]{1,0,2:T(1,128)}, f32[1,1024,60]{1,0,2:T(1,128)S(1)}, u32[]{:S(2)}) copy-start(f32[1,1024,60]{1,0,2:T(1,128)S(1)} %constant_dynamic-update-slice_fusion) | copy-start | bytes 737284
  25.8 1.2 copy-start.1
  33.0 8.6 %copy-start.2 = (bf16[5,384,384]{2,1,0:T(8,128)(2,1)S(1)}, bf16[5,384,384]{2,1,0:T(8,128)(2,1)}, u32[]{:S(2)}) copy-start(bf16[5,384,384]{2,1,0:T(8,128)(2,1)} %param.14) | copy-start | bytes 4423684
  34.8 8.7 %copy-start.5 = (bf16[1,512,384]{2,1,0:T(8,128)(2,1)}, bf16[1,512,384]{2,1,0:T(8,128)(2,1)S(1)}, u32[]{:S(2)}) copy-start(bf16[1,512,384]{2,1,0:T(8,128)(2,1)S(1)} %get-tuple-element.33) | copy-start | bytes 1179652
  34.9 18.5 %collective-permute-start.3 = (bf16[1,2,384]{2,1,0:T(2,128)(2,1)S(1)}, bf16[1,2,384]{2,1,0:T(2,128)(2,1)S(1)}, u32[]{:S(2)}, u32[]{:S(2)}) collective-permute-start(bf16[1,2,384]{2,1,0:T(2,128)(2,1)S(1)} %get-tuple-element.44), channel_id=1, source_target_pairs={{1,0},{2,1},{3,2},{4,3},{5,4},{6,5},{7,6},{8,7},{9,8},{10,9},{11,1... | collective-permute-start | bytes 4616 | tf_op jit(solution)/shard_map/ppermute | solution.py:307
  36.8 15.3 %collective-permute-start.2 = (bf16[1,2,384]{2,1,0:T(2,128)(2,1)S(1)}, bf16[1,2,384]{2,1,0:T(2,128)(2,1)S(1)}, u32[]{:S(2)}, u32[]{:S(2)}) collective-permute-start(bf16[1,2,384]{2,1,0:T(2,128)(2,1)S(1)} %get-tuple-element.45), channel_id=1, source_target_pairs={{0,1},{1,2},{2,3},{3,4},{4,5},{5,6},{6,7},{7,8},{8,9},{9,10},{10,1... | collective-permute-start | bytes 4616 | tf_op jit(solution)/shard_map/ppermute | solution.py:304
  41.6 1.1 copy-start.4
  45.7 2.2 %copy-start.14 = (f32[1,1024,60]{1,0,2:T(1,128)S(1)}, f32[1,1024,60]{1,0,2:T(1,128)}, u32[]{:S(2)}) copy-start(f32[1,1024,60]{1,0,2:T(1,128)} %copy-done.13) | copy-start | bytes 737284
  48.0 4.1 %copy-start.3 = (bf16[5,384,384]{2,1,0:T(8,128)(2,1)S(1)}, bf16[5,384,384]{2,1,0:T(8,128)(2,1)}, u32[]{:S(2)}) copy-start(bf16[5,384,384]{2,1,0:T(8,128)(2,1)} %param.14) | copy-start | bytes 4423684
  52.1 0.8 copy-start.11
  61.3 1.5 %copy-start.10 = (bf16[384,512]{1,0:T(8,128)(2,1)S(1)}, bf16[384,512]{1,0:T(8,128)(2,1)}, u32[]{:S(2)}) copy-start(bf16[384,512]{1,0:T(8,128)(2,1)} %copy.39) | copy-start | bytes 1179652
  61.3 1.9 %copy-start.7 = (bf16[384,512]{1,0:T(8,128)(2,1)S(1)}, bf16[384,512]{1,0:T(8,128)(2,1)}, u32[]{:S(2)}) copy-start(bf16[384,512]{1,0:T(8,128)(2,1)} %copy.40) | copy-start | bytes 1179652
  62.7 1.0 copy-start.9
  63.1 1.0 copy-start.8
  64.6 0.9 copy-start.12
  127.0 1.0 copy-start.6

commit v2 on v1

v2 whole, which is shorter than its diff:
```python
import functools
import math

import jax
import jax.numpy as jnp
from jax import lax
from jax.experimental import pallas as pl
from jax.experimental.pallas import tpu as pltpu
from jax.sharding import PartitionSpec as P

MESH = pl.DeviceIdType.MESH
f32, bf16 = jnp.float32, jnp.bfloat16
root_scale = math.sqrt(2.0 / math.pi)
cubic = 0.044715

C = 384
ROWS = 512
LEAD = 16
TALL = ROWS + 2 * LEAD
LANES = 640
PAIRS = 44


def places(ring, deep, high):
    low = ring // high
    dp, ctx = lax.axis_index("dp"), lax.axis_index("context")
    y, xh = lax.div(dp, high), lax.rem(dp, high)
    core, z = lax.rem(ctx, 2), lax.rem(lax.div(ctx, 2), deep)
    x = xh * low + lax.div(ctx, 2 * deep)

    def device(x, y, z, core):
        return {
            "dp": y * high + lax.div(x, low),
            "context": (lax.rem(x, low) * deep + z) * 2 + core,
        }

    return x, y, z, core, device


def remote(src, dst, send, recv, to):
    return pltpu.make_async_remote_copy(
        src_ref=src, dst_ref=dst, send_sem=send, recv_sem=recv, device_id=to, device_id_type=MESH
    )


def halo_kernel(count, codes, cot, near_codes, near_cot, sends, recvs):
    ctx = lax.axis_index("context")
    left = {"context": lax.rem(ctx + count - 1, count)}
    right = {"context": lax.rem(ctx + 1, count)}
    barrier = pltpu.get_barrier_semaphore()
    for to in (left, right):
        pl.semaphore_signal(barrier, inc=1, device_id=to, device_id_type=MESH)
    pl.semaphore_wait(barrier, 2)
    copies = [
        remote(codes, near_codes.at[0], sends.at[0], recvs.at[0], right),
        remote(codes, near_codes.at[1], sends.at[1], recvs.at[1], left),
        remote(cot.at[ROWS - LEAD : ROWS], near_cot.at[0], sends.at[2], recvs.at[2], right),
        remote(cot.at[0:LEAD], near_cot.at[1], sends.at[3], recvs.at[3], left),
    ]
    for copy in copies:
        copy.start()
    for copy in copies:
        copy.wait()


def halo(count, codes, cot):
    return pl.pallas_call(
        functools.partial(halo_kernel, count),
        out_shape=(
            jax.ShapeDtypeStruct((2, 8, 128), jnp.int32),
            jax.ShapeDtypeStruct((2, LEAD, C), bf16),
        ),
        in_specs=[pl.BlockSpec(memory_space=pltpu.VMEM)] * 2,
        out_specs=(pl.BlockSpec(memory_space=pltpu.VMEM),) * 2,
        scratch_shapes=[pltpu.SemaphoreType.DMA((4,)), pltpu.SemaphoreType.DMA((4,))],
        compiler_params=pltpu.CompilerParams(collective_id=0, has_side_effects=True),
        name="halo",
    )(codes, cot)


def main_kernel(
    ring, deep, high, count,
    vpos, vshift, codes, near_codes, cot, near_cot, stem_weight, weight,
    features, d_pooled, gathered, stem_all,
    wt, wf, wsem, ws, stem, slopes, cotx, gx, pooled, pslope, shifted, spread, wins_t, gated_t, dstem,
    own, s0, r0, s1, r1, a2, s2, r2,
    t0, u0, tsum, t1, u1, t2, u2,
    v3, s3, r3, g3, w3,
    c0s, c0r, c1s, c1r, c2s, c2r, c3s, c3r, d3s, d3r, d2s, d2r, d1s, d1r, d0s, d0r,
    e0s, e0r, e1s, e1r, e2s, e2r, h0s, h0r,
):
    x, y, z, core, device = places(ring, deep, high)
    ctx = lax.axis_index("context")
    other = 1 - core
    per = 4 // ring
    rows1 = per * C
    rows2 = rows1 // ring

    def along(half, level, step):
        if (half == 0) == (level == 1):
            return device(lax.rem(x + step, ring), y, z, core)
        return device(x, lax.rem(y + step, ring), z, core)

    def mine(half, level):
        return x if (half == 0) == (level == 1) else y

    def deeper(step):
        return device(x, y, lax.rem(z + step, deep), core)

    sibling = device(x, y, z, other)
    order = sorted(range(1, ring), key=lambda d: -min(d, ring - d))
    near = order[::-1]

    barrier = pltpu.get_barrier_semaphore()
    pl.semaphore_signal(barrier, inc=1, device_id=sibling, device_id_type=MESH)

    def greet(step, carry):
        pl.semaphore_signal(barrier, inc=1, device_id=deeper(step), device_id_type=MESH)
        return carry

    lax.fori_loop(1, deep, greet, 0)
    for step in range(1, ring):
        for half in range(2):
            pl.semaphore_signal(barrier, inc=1, device_id=along(half, 1, step), device_id_type=MESH)

    loads = [pltpu.make_async_copy(weight.at[t], wt.at[:, t * C : (t + 1) * C], wsem.at[t]) for t in range(5)]
    loads += [pltpu.make_async_copy(weight.at[t], wf.at[t * C : (t + 1) * C], wsem.at[5 + t]) for t in range(5)]
    for load in loads:
        load.start()

    bases = jnp.concatenate(
        [near_codes[0, 7:8], codes[...], near_codes[1, 0:1], jnp.zeros((6, 128), jnp.int32)], axis=0
    )
    spot = (
        ctx * (2 * ROWS) - 128
        + 128 * lax.broadcasted_iota(jnp.int32, (16, 128), 0)
        + lax.broadcasted_iota(jnp.int32, (16, 128), 1)
    )
    for v in range(vpos.shape[1]):
        bases = bases + jnp.where(spot == vpos[0, v], vshift[0, v], 0)
    bases = jnp.where((spot >= 0) & (spot < count * (2 * ROWS)), bases & 3, 4)
    lane_in = lax.broadcasted_iota(jnp.int32, (128, 128), 0)
    lane_out = lax.broadcasted_iota(jnp.int32, (128, 128), 1)
    pick = (lane_in == 2 * (lane_out & 63) + lax.shift_right_logical(lane_out, 6)).astype(f32).astype(bf16)
    split = jnp.dot(bases.astype(f32).astype(bf16), pick, preferred_element_type=f32)
    turned = pltpu.roll(split, 64, 1)
    first = lax.broadcasted_iota(jnp.int32, (1, 128), 1) < 64
    evens, odds = [], []
    for p in range(5):
        evens.append(jnp.where(first, split[2 * p : 2 * p + 1], turned[2 * p + 1 : 2 * p + 2]))
        odds.append(jnp.where(first, turned[2 * p : 2 * p + 1], split[2 * p + 1 : 2 * p + 2]))
    even = jnp.broadcast_to(jnp.concatenate(evens, axis=1), (8, LANES))
    odd = jnp.broadcast_to(jnp.concatenate(odds, axis=1), (8, LANES))
    line = lax.broadcasted_iota(jnp.int32, (8, LANES), 0)
    both = jnp.where(line < 4, odd, pltpu.roll(even, LANES - 1, 1))
    hot = (both == (line & 3).astype(f32)).astype(f32)
    wide = [pltpu.roll(hot, LANES - (PAIRS + q), 1) for q in range(8)]
    windows_t = jnp.concatenate(wide + wide, axis=0)
    windows = windows_t.T[:TALL].astype(bf16)
    kept = jnp.concatenate(
        [pltpu.roll(hot, LANES - (PAIRS + LEAD + q), 1)[:, :ROWS] for q in range(8)], axis=0
    )
    wins_t[...] = kept.astype(bf16)

    ws[...] = jnp.zeros_like(ws)
    for k in range(15):
        ws[4 * k : 4 * k + 4, 0:C] = stem_weight[k]
        ws[4 * k + 4 : 4 * k + 8, C:] = stem_weight[k]
    taps = ws[...]
    upper = taps.astype(bf16)
    lower = (taps - upper.astype(f32)).astype(bf16)
    stem[...] = jnp.dot(windows, jnp.concatenate([upper, lower], axis=0), preferred_element_type=f32)

    def bend(value):
        square = value * value
        inner = jnp.tanh(value * (root_scale + (root_scale * cubic) * square))
        active = 0.5 * value * (1.0 + inner)
        slope = 0.5 * (1.0 + inner) + 0.5 * value * (1.0 - inner * inner) * (
            root_scale + (3.0 * root_scale * cubic) * square
        )
        return active, slope

    def activate(i, carry):
        rows = pl.ds(pl.multiple_of(i * 16, 16), 16)
        active_e, slope_e = bend(stem[rows, 0:C])
        active_o, slope_o = bend(stem[rows, C:])
        slopes[rows, 0:C] = 0.5 * slope_e
        slopes[rows, C:] = 0.5 * slope_o
        pool = (0.5 * (active_e + active_o)).astype(bf16).astype(f32)
        pooled[rows] = pool
        gate, slope = bend(pool)
        gx[rows] = gate.astype(bf16).astype(f32)
        pslope[rows] = slope
        return carry

    lax.fori_loop(0, TALL // 16, activate, 0)
    inside_left = jnp.where(ctx > 0, 1.0, 0.0)
    inside_right = jnp.where(ctx < count - 1, 1.0, 0.0)
    gx[0:LEAD] = gx[0:LEAD] * inside_left
    gx[LEAD + ROWS :] = gx[LEAD + ROWS :] * inside_right
    cotx[0:LEAD] = near_cot[0].astype(f32) * inside_left
    cotx[LEAD + ROWS :] = near_cot[1].astype(f32) * inside_right
    cotx[LEAD : LEAD + ROWS] = cot[...].astype(f32)
    gated_t[...] = gx[LEAD : LEAD + ROWS].T.astype(bf16)
    for t in range(5):
        shifted[:, t * C : (t + 1) * C] = cotx[LEAD + 2 - t : LEAD + 2 - t + ROWS].astype(bf16)
    shifted[:, 5 * C :] = jnp.zeros((ROWS, 128), bf16)

    pl.semaphore_wait(barrier, 1 + 2 * (ring - 1) + deep - 1)

    def level0(half, piece):
        return remote(
            s0.at[half, piece], r0.at[half, piece], c0s.at[half, piece], c0r.at[half, piece], sibling
        )

    def product(owner, j):
        at = pl.multiple_of(owner * 1024 + 256 * j, 256)
        return jnp.dot(gated_t[...], shifted[:, pl.ds(at, 256)], preferred_element_type=f32)

    for j in range(4):
        block = product(other, j)
        for k in range(2):
            half, sub = divmod(2 * j + k, 4)
            piece, sub = divmod(sub, per)
            s0[half, piece, sub * C : (sub + 1) * C] = block[:, 128 * k : 128 * (k + 1)].astype(bf16)
            if sub == per - 1:
                level0(half, piece).start()
    for j in range(4):
        block = product(core, j)
        for k in range(2):
            half, sub = divmod(2 * j + k, 4)
            piece, sub = divmod(sub, per)
            own[half, piece, sub * C : (sub + 1) * C] = block[:, 128 * k : 128 * (k + 1)]

    def level1(half, step):
        return remote(
            s1.at[half, step - 1], r1.at[half, step - 1], c1s.at[half, step - 1], c1r.at[half, step - 1],
            along(half, 1, step),
        )

    for half in range(2):
        for piece in range(ring):
            level0(half, piece).wait_recv()
    for step in order:
        for half in range(2):
            piece = lax.rem(mine(half, 1) + step, ring)
            s1[half, step - 1] = (own[half, piece] + r0[half, piece].astype(f32)).astype(bf16)
            level1(half, step).start()

    for load in loads:
        load.wait()
    for block in range(2):
        at = block * (ROWS // 2)
        rows = slice(at, at + ROWS // 2)
        more = slice(LEAD + at, LEAD + at + ROWS // 2)
        back = lax.dot_general(
            shifted[rows, : 5 * C], wt[...], (((1,), (1,)), ((), ())), preferred_element_type=f32
        )
        dpool = cotx[more] + back * pslope[more]
        d_pooled[rows] = dpool.astype(bf16)
        dstem[rows, 0:C] = (dpool * slopes[more, 0:C]).astype(bf16)
        dstem[rows, C:] = (dpool * slopes[more, C:]).astype(bf16)
    grad = jnp.dot(wins_t[...], dstem[...], preferred_element_type=f32)
    for k in range(3):
        tsum[k * 64 : k * 64 + 64] = grad[:, 128 * k : 128 * (k + 1)]
    for k in range(3):
        tsum[k * 64 : k * 64 + 60] = tsum[k * 64 : k * 64 + 60] + grad[4:64, C + 128 * k : C + 128 * (k + 1)]

    def stem0():
        return remote(t0, u0, e0s, e0r, sibling)

    t0[...] = tsum[pl.ds(pl.multiple_of(other * 96, 96), 96)].astype(bf16)
    stem0().start()

    for t in range(5):
        spread[:, t * C : (t + 1) * C] = gx[LEAD - 2 + t : LEAD - 2 + t + ROWS].astype(bf16)
    for block in range(2):
        at = block * (ROWS // 2)
        rows = slice(at, at + ROWS // 2)
        conv = jnp.dot(spread[rows], wf[...], preferred_element_type=f32)
        features[rows] = (pooled[LEAD + at : LEAD + at + ROWS // 2] + conv).astype(bf16)

    def stem1(step):
        return remote(t1, u1.at[step - 1], e1s.at[step - 1], e1r.at[step - 1], along(0, 1, step))

    def stem2(step):
        return remote(t2, u2.at[step - 1], e2s.at[step - 1], e2r.at[step - 1], along(0, 2, step))

    stem0().wait_recv()
    small = tsum[pl.ds(pl.multiple_of(core * 96, 96), 96)] + u0[...].astype(f32)
    t1[...] = small.astype(bf16)
    for step in order:
        stem1(step).start()

    def level2(half, step):
        return remote(
            s2.at[half, lax.rem(mine(half, 2) + step, ring)], r2.at[half, step - 1],
            c2s.at[half, step - 1], c2r.at[half, step - 1], along(half, 2, step),
        )

    for half in range(2):
        piece = mine(half, 1)
        total = own[half, piece] + r0[half, piece].astype(f32)
        for step in range(1, ring):
            level1(half, step).wait_recv()
            total = total + r1[half, step - 1].astype(f32)
        total = total.reshape(a2.shape[1:])
        a2[half] = total
        s2[half] = total.astype(bf16)
        for step in order:
            level2(half, step).start()

    for step in range(1, ring):
        stem1(step).wait_recv()
        small = small + u1[step - 1].astype(f32)
    t2[...] = small.astype(bf16)
    for step in order:
        stem2(step).start()

    for half in range(2):
        total = a2[half, mine(half, 2)]
        for step in range(1, ring):
            level2(half, step).wait_recv()
            total = total + r2[half, step - 1].astype(f32)
        v3[half * rows2 : (half + 1) * rows2] = total
    for step in range(1, ring):
        stem2(step).wait_recv()
        small = small + u2[step - 1].astype(f32)
    v3[2 * rows2 : 2 * rows2 + 96] = small
    share = (2 * rows2 + 96) // deep
    tall = s3.shape[1]
    for piece in range(deep):
        s3[piece] = v3[piece * share : piece * share + tall].astype(bf16)

    def level3(step):
        return remote(
            s3.at[lax.rem(z + step, deep)], r3.at[step - 1], c3s.at[step - 1], c3r.at[step - 1], deeper(step)
        )

    def back3(step):
        return remote(g3.at[z], g3.at[z], d3s.at[step - 1], d3r.at[step - 1], deeper(step))

    def far(i):
        half_way = deep // 2 - lax.div(i + 1, 2)
        return jnp.where(lax.rem(i, 2) == 0, half_way, deep - half_way)

    def send3(i, carry):
        level3(far(i)).start()
        return carry

    lax.fori_loop(0, deep - 1, send3, 0)

    def take3(i, total):
        level3(i + 1).wait_recv()
        return total + r3[i].astype(f32)

    g3[z] = lax.fori_loop(0, deep - 1, take3, s3[z].astype(f32)).astype(bf16)

    def spread3(i, carry):
        back3(far(i)).start()
        return carry

    lax.fori_loop(0, deep - 1, spread3, 0)

    def got3(i, carry):
        back3(i + 1).wait_recv()
        return carry

    lax.fori_loop(0, deep - 1, got3, 0)
    for piece in range(deep):
        w3[piece * share : piece * share + tall] = g3[piece].astype(f32)

    def back2(half, step):
        spot = gathered.at[core, half, mine(half, 1), mine(half, 2)]
        return remote(spot, spot, d2s.at[half, step - 1], d2r.at[half, step - 1], along(half, 2, step))

    for half in range(2):
        gathered[core, half, mine(half, 1), mine(half, 2)] = w3[half * rows2 : (half + 1) * rows2].astype(bf16)
        for step in order:
            back2(half, step).start()

    def back_stem():
        return remote(stem_all.at[core], stem_all.at[core], h0s, h0r, sibling)

    stem_all[core] = w3[2 * rows2 : 2 * rows2 + 96].astype(bf16)
    back_stem().start()

    def back1(half, step):
        spot = gathered.at[core, half, mine(half, 1)]
        return remote(spot, spot, d1s.at[half, step - 1], d1r.at[half, step - 1], along(half, 1, step))

    def back0(half, step):
        spot = gathered.at[core, half, lax.rem(mine(half, 1) + ring - step, ring)]
        return remote(spot, spot, d0s.at[half, step], d0r.at[half, step], sibling)

    for half in range(2):
        for step in range(1, ring):
            back2(half, step).wait_recv()
        for step in order:
            back1(half, step).start()
        back0(half, 0).start()
    for step in near:
        for half in range(2):
            back1(half, step).wait_recv()
            back0(half, step).start()
    back_stem().wait()
    stem0().wait_send()
    for half in range(2):
        for step in range(ring):
            back0(half, step).wait()
            level0(half, step).wait_send()
        for step in range(1, ring):
            level1(half, step).wait_send()
            level2(half, step).wait_send()
            back2(half, step).wait_send()
            back1(half, step).wait_send()
    for step in range(1, ring):
        stem1(step).wait_send()
        stem2(step).wait_send()

    def sent3(i, carry):
        level3(i + 1).wait_send()
        back3(i + 1).wait_send()
        return carry

    lax.fori_loop(0, deep - 1, sent3, 0)


def main(ring, deep, high, vpos, vshift, codes, near_codes, cot, near_cot, stem_weight, weight):
    per = 4 // ring
    rows1 = per * C
    rows2 = rows1 // ring
    share = (2 * rows2 + 96) // deep
    tall = -(-share // 8) * 8
    count = 2 * (ring // high) * deep
    dma = pltpu.SemaphoreType.DMA
    halves = lambda *lead: pltpu.VMEM((2,) + lead, bf16)
    pair = lambda *dims: [dma(dims), dma(dims)]
    vmem = pl.BlockSpec(memory_space=pltpu.VMEM)
    smem = pl.BlockSpec(memory_space=pltpu.SMEM)
    return pl.pallas_call(
        functools.partial(main_kernel, ring, deep, high, count),
        out_shape=(
            jax.ShapeDtypeStruct((ROWS, C), bf16),
            jax.ShapeDtypeStruct((ROWS, C), bf16),
            jax.ShapeDtypeStruct((2, 2, ring, ring, rows2, 128), bf16),
            jax.ShapeDtypeStruct((2, 96, 128), bf16),
        ),
        in_specs=[smem, smem, vmem, vmem, vmem, vmem, vmem, pl.BlockSpec(memory_space=pl.ANY)],
        out_specs=(vmem,) * 4,
        scratch_shapes=[
            pltpu.VMEM((C, 5 * C), bf16),
            pltpu.VMEM((5 * C, C), bf16),
            dma((10,)),
            pltpu.VMEM((64, 2 * C), f32),
            pltpu.VMEM((TALL, 2 * C), f32),
            pltpu.VMEM((TALL, 2 * C), f32),
            pltpu.VMEM((TALL, C), f32),
            pltpu.VMEM((TALL, C), f32),
            pltpu.VMEM((TALL, C), f32),
            pltpu.VMEM((TALL, C), f32),
            pltpu.VMEM((ROWS, 2048), bf16),
            pltpu.VMEM((ROWS, 5 * C), bf16),
            pltpu.VMEM((64, ROWS), bf16),
            pltpu.VMEM((C, ROWS), bf16),
            pltpu.VMEM((ROWS, 2 * C), bf16),
            pltpu.VMEM((2, ring, rows1, 128), f32),
            halves(ring, rows1, 128),
            halves(ring, rows1, 128),
            halves(ring - 1, rows1, 128),
            halves(ring - 1, rows1, 128),
            pltpu.VMEM((2, ring, rows2, 128), f32),
            halves(ring, rows2, 128),
            halves(ring - 1, rows2, 128),
            pltpu.VMEM((96, 128), bf16),
            pltpu.VMEM((96, 128), bf16),
            pltpu.VMEM((192, 128), f32),
            pltpu.VMEM((96, 128), bf16),
            pltpu.VMEM((ring - 1, 96, 128), bf16),
            pltpu.VMEM((96, 128), bf16),
            pltpu.VMEM((ring - 1, 96, 128), bf16),
            pltpu.VMEM((2 * rows2 + 96 + tall, 128), f32),
            pltpu.VMEM((deep, tall, 128), bf16),
            pltpu.VMEM((deep - 1, tall, 128), bf16),
            pltpu.VMEM((deep, tall, 128), bf16),
            pltpu.VMEM((2 * rows2 + 96 + tall, 128), f32),
            *pair(2, ring), *pair(2, ring - 1), *pair(2, ring - 1), *pair(deep - 1),
            *pair(deep - 1), *pair(2, ring - 1), *pair(2, ring - 1), *pair(2, ring),
            *pair(), *pair(ring - 1), *pair(ring - 1), *pair(),
        ],
        compiler_params=pltpu.CompilerParams(
            collective_id=1, has_side_effects=True, vmem_limit_bytes=60 * 1024 * 1024
        ),
        name="block",
    )(vpos, vshift, codes, near_codes, cot, near_cot, stem_weight, weight)


def finish_kernel(summed, small, conv, stem):
    t = pl.program_id(0)
    for k in range(3):
        conv[0, :, k * 128 : (k + 1) * 128] = summed[3 * t + k].astype(f32)

    @pl.when(t == 0)
    def _():
        rows = jnp.concatenate([small[0], small[1]], axis=0).astype(f32)
        for k in range(3):
            for tap in range(15):
                stem[tap, :, k * 128 : (k + 1) * 128] = rows[k * 64 + 4 * tap : k * 64 + 4 * tap + 4]


def finish(summed, small):
    vmem = pl.BlockSpec(memory_space=pltpu.VMEM)
    return pl.pallas_call(
        finish_kernel,
        grid=(5,),
        out_shape=(
            jax.ShapeDtypeStruct((5, C, C), f32),
            jax.ShapeDtypeStruct((15, 4, C), f32),
        ),
        in_specs=[vmem, vmem],
        out_specs=(
            pl.BlockSpec((1, C, C), lambda t: (t, 0, 0)),
            pl.BlockSpec((15, 4, C), lambda t: (0, 0, 0)),
        ),
        name="finish",
    )(summed.reshape(16, C, 128), small)


def per_device(ring, deep, high, codes, variant_pos, variant_shift, stem_weight, conv_weight, cotangent):
    codes = codes.reshape(8, 128)
    cot = cotangent.reshape(ROWS, C)
    near_codes, near_cot = halo(2 * (ring // high) * deep, codes, cot)
    features, d_pooled, summed, small = main(
        ring, deep, high, variant_pos, variant_shift, codes, near_codes, cot, near_cot, stem_weight, conv_weight
    )
    conv_grad, stem_grad = finish(summed, small)
    return features[None], d_pooled[None], conv_grad, stem_grad


def build(mesh, ring, deep, high):
    placed = (P("dp", "context"), P("dp", None), P("dp", None), P(), P(), P("dp", "context", None))
    return jax.shard_map(
        functools.partial(per_device, ring, deep, high),
        mesh=mesh,
        in_specs=placed,
        out_specs=(P("dp", "context", None), P("dp", "context", None), P(), P()),
        check_vma=False,
    )


def solution(mesh):
    return build(mesh, 4, 16, 2)
```

time: 130 us -> 76 us (0.58)
  local copies, waits for them, and re-layouts: 24.3 us -> 1.5 us
  starting transfers between devices: 20.7 us -> 0 us
  matrix products: 16.3 us -> 0 us
  Pallas kernels: 59.6 us -> 73.7 us
  other arithmetic: 7.03 us -> 0 us
    ppermute x6 -> x0, starting transfers between devices: 20.7 us -> none  [the longest x3 13.1 us: with_halo(): lax.ppermute(lax.slice_in_dim(block, 0, width, axis=dim), axis, backward)]
    dot_general x17 -> x0, matrix products: 16.3 us -> none  [the longest x5 5.11 us: per_device(): jnp.einsum('brd,cd->brc', cot_ext[:, 4 - offset:4 - offset + half_rows],...]
    pallas_call x1 -> x2, Pallas kernels: 55.5 us -> 69.6 us  [the longest x1 55.2 us: main(): pl.pallas_call(functools.partial(main_kernel, ring, deep, high, count), o...]
    dot_general x5 -> x0, local copies, waits for them, and re-layouts: 7.65 us -> none  [per_device(): jnp.einsum('brc,brd->cd', gated_ext[:, offset:offset + half_rows], cotang...]
    slice x5 -> x0, local copies, waits for them, and re-layouts: 6.36 us -> none  [the longest x2 5.56 us: per_device(): pooled = (0.5 * (active[:, 0::2] + active[:, 1::2])).astype(jnp.bfloat16)]
    unnamed x48 -> x6, local copies, waits for them, and re-layouts: 6.91 us -> 1.5 us
    mul x1 -> x0, local copies, waits for them, and re-layouts: 2.22 us -> none  [per_device(): dstem = 0.5 * jnp.repeat(dpool, 2, axis=1) * gelu_slope(stem)]
    convert_element_type x2 -> x0, other arithmetic: 1.92 us -> none  [the longest x1 1.84 us: per_device(): gated = gelu_tanh(pooled_f).astype(jnp.bfloat16)]
  transfers between devices with their start and end apart: 6 -> 0, of which waited for: 0 -> 0; matrix products, arithmetic and copies ran while one was open for 22% -> 0% of each run, Pallas kernels for 0% -> 0%
where the time goes in v2:
time: 76 us; the launch traced here: 75.8 us
  Pallas kernels  73.7 us (97%)
  local copies, waits for them, and re-layouts  1.5 us (2%)
    pallas_call x1, Pallas kernels, main(): pl.pallas_call(functools.partial(main_kernel, ring, deep, high, count), o...  55.2 us
    pallas_call x1, Pallas kernels, halo(): pl.pallas_call(functools.partial(halo_kernel, count), out_shape=(jax.Shap...  14.4 us
    pallas_call x1, Pallas kernels, finish(): pl.pallas_call(finish_kernel, grid=(5,), out_shape=(jax.ShapeDtypeStruct(...  4.09 us

profile of v2, /device:TPU:1, one launch (start us, length us, event | category | flops | bytes accessed | tf_op | source)
XLA Modules:
  0.0 75.8 jit_solution(6330118743627422072)
XLA Ops:
  0.6 14.4 %halo.1 = (s32[2,8,128]{2,1,0:T(8,128)}, bf16[2,16,384]{2,1,0:T(8,128)(2,1)}) custom-call(s32[8,128]{1,0:T(8,128)} %bitcast.10, bf16[512,384]{1,0:T(8,128)(2,1)} %bitcast.6), custom_call_target="tpu_custom_call" | custom-call | tf_op jit(solution)/shard_map/halo/pallas_call | solution.py:67
  15.0 55.2 %block.1 = (bf16[512,384]{1,0:T(8,128)(2,1)}, bf16[512,384]{1,0:T(8,128)(2,1)}, bf16[2,2,4,4,96,128]{5,4,3,2,1,0:T(8,128)(2,1)}, bf16[2,96,128]{2,1,0:T(8,128)(2,1)}) custom-call(s32[1,64]{1,0:T(1,128)} %vpos.1, s32[1,64]{1,0:T(1,128)} %vshift.1, s32[8,128]{1,0:T(8,128)} %bitcast.11, s32[2,8,128]{2,1,0:T(8,128)} %get-tuple-element.12.near_codes, ...), custom_call_target="tpu_custom_call" | custom-call | tf_op jit(solution)/shard_map/block/pallas_call | solution.py:441
  70.2 0.0 copy-start.1
  70.2 0.0 copy-start
  70.2 4.1 %finish.1 = (f32[5,384,384]{2,1,0:T(8,128)}, f32[15,4,384]{2,1,0:T(4,128)}) custom-call(bf16[16,384,128]{2,1,0:T(8,128)(2,1)} %bitcast.5, bf16[2,96,128]{2,1,0:T(8,128)(2,1)} %get-tuple-element.17.small), custom_call_target="tpu_custom_call" | custom-call | tf_op jit(solution)/shard_map/finish/pallas_call | solution.py:513
  74.3 0.0 copy-done.1
  74.3 0.7 copy.12
  75.1 0.0 copy-done
  75.1 0.7 copy.13
Async XLA Ops:
  70.2 4.1 %copy-start.1 = (bf16[512,384]{1,0:T(8,128)(2,1)S(1)}, bf16[512,384]{1,0:T(8,128)(2,1)}, u32[]{:S(2)}) copy-start(bf16[512,384]{1,0:T(8,128)(2,1)} %get-tuple-element.14) | copy-start | bytes 1179652
  70.2 4.9 %copy-start = (bf16[512,384]{1,0:T(8,128)(2,1)S(1)}, bf16[512,384]{1,0:T(8,128)(2,1)}, u32[]{:S(2)}) copy-start(bf16[512,384]{1,0:T(8,128)(2,1)} %get-tuple-element.15) | copy-start | bytes 1179652

commit v3 on v2

--- a/solution.py
+++ b/solution.py
@@ -70,18 +70,21 @@
             jax.ShapeDtypeStruct((2, 8, 128), jnp.int32),
             jax.ShapeDtypeStruct((2, LEAD, C), bf16),
         ),
-        in_specs=[pl.BlockSpec(memory_space=pltpu.VMEM)] * 2,
+        in_specs=[pl.BlockSpec(memory_space=pltpu.HBM)] * 2,
         out_specs=(pl.BlockSpec(memory_space=pltpu.VMEM),) * 2,
         scratch_shapes=[pltpu.SemaphoreType.DMA((4,)), pltpu.SemaphoreType.DMA((4,))],
-        compiler_params=pltpu.CompilerParams(collective_id=0, has_side_effects=True),
+        compiler_params=pltpu.CompilerParams(
+            collective_id=0, has_side_effects=True, vmem_limit_bytes=2 * 1024 * 1024
+        ),
         name="halo",
     )(codes, cot)
 
 
 def main_kernel(
     ring, deep, high, count,
-    vpos, vshift, codes, near_codes, cot, near_cot, stem_weight, weight,
+    vpos_in, vshift_in, codes_in, near_codes, cot_in, near_cot, stem_weight_in, weight,
     features, d_pooled, gathered, stem_all,
+    vpos, vshift, codes, cot, stem_weight, insem,
     wt, wf, wsem, ws, stem, slopes, cotx, gx, pooled, pslope, shifted, spread, wins_t, gated_t, dstem,
     own, s0, r0, s1, r1, a2, s2, r2,
     t0, u0, tsum, t1, u1, t2, u2,
@@ -111,6 +114,14 @@
     order = sorted(range(1, ring), key=lambda d: -min(d, ring - d))
     near = order[::-1]
 
+    feeds = [
+        pltpu.make_async_copy(source, target, insem.at[i])
+        for i, (source, target) in enumerate(
+            [(vpos_in, vpos), (vshift_in, vshift), (codes_in, codes), (stem_weight_in, stem_weight), (cot_in, cot)]
+        )
+    ]
+    for feed in feeds:
+        feed.start()
     barrier = pltpu.get_barrier_semaphore()
     pl.semaphore_signal(barrier, inc=1, device_id=sibling, device_id_type=MESH)
 
@@ -128,6 +139,8 @@
     for load in loads:
         load.start()
 
+    for feed in feeds[:3]:
+        feed.wait()
     bases = jnp.concatenate(
         [near_codes[0, 7:8], codes[...], near_codes[1, 0:1], jnp.zeros((6, 128), jnp.int32)], axis=0
     )
@@ -162,6 +175,7 @@
     )
     wins_t[...] = kept.astype(bf16)
 
+    feeds[3].wait()
     ws[...] = jnp.zeros_like(ws)
     for k in range(15):
         ws[4 * k : 4 * k + 4, 0:C] = stem_weight[k]
@@ -200,6 +214,7 @@
     gx[LEAD + ROWS :] = gx[LEAD + ROWS :] * inside_right
     cotx[0:LEAD] = near_cot[0].astype(f32) * inside_left
     cotx[LEAD + ROWS :] = near_cot[1].astype(f32) * inside_right
+    feeds[4].wait()
     cotx[LEAD : LEAD + ROWS] = cot[...].astype(f32)
     gated_t[...] = gx[LEAD : LEAD + ROWS].T.astype(bf16)
     for t in range(5):
@@ -437,7 +452,7 @@
     halves = lambda *lead: pltpu.VMEM((2,) + lead, bf16)
     pair = lambda *dims: [dma(dims), dma(dims)]
     vmem = pl.BlockSpec(memory_space=pltpu.VMEM)
-    smem = pl.BlockSpec(memory_space=pltpu.SMEM)
+    hbm = pl.BlockSpec(memory_space=pltpu.HBM)
     return pl.pallas_call(
         functools.partial(main_kernel, ring, deep, high, count),
         out_shape=(
@@ -446,9 +461,15 @@
             jax.ShapeDtypeStruct((2, 2, ring, ring, rows2, 128), bf16),
             jax.ShapeDtypeStruct((2, 96, 128), bf16),
         ),
-        in_specs=[smem, smem, vmem, vmem, vmem, vmem, vmem, pl.BlockSpec(memory_space=pl.ANY)],
+        in_specs=[hbm, hbm, hbm, vmem, hbm, vmem, hbm, hbm],
         out_specs=(vmem,) * 4,
         scratch_shapes=[
+            pltpu.SMEM(vpos.shape, jnp.int32),
+            pltpu.SMEM(vshift.shape, jnp.int32),
+            pltpu.VMEM((8, 128), jnp.int32),
+            pltpu.VMEM((ROWS, C), bf16),
+            pltpu.VMEM((15, 4, C), f32),
+            dma((5,)),
             pltpu.VMEM((C, 5 * C), bf16),
             pltpu.VMEM((5 * C, C), bf16),
             dma((10,)),
@@ -489,51 +510,63 @@
             *pair(), *pair(ring - 1), *pair(ring - 1), *pair(),
         ],
         compiler_params=pltpu.CompilerParams(
-            collective_id=1, has_side_effects=True, vmem_limit_bytes=60 * 1024 * 1024
+            collective_id=1, has_side_effects=True, vmem_limit_bytes=36 * 1024 * 1024
         ),
         name="block",
     )(vpos, vshift, codes, near_codes, cot, near_cot, stem_weight, weight)
 
 
-def finish_kernel(summed, small, conv, stem):
-    t = pl.program_id(0)
+def finish_kernel(summed, small, features, d_pooled, conv, stem, features_out, d_pooled_out, widened, sems):
+    copies = [
+        pltpu.make_async_copy(features, features_out, sems.at[5]),
+        pltpu.make_async_copy(d_pooled, d_pooled_out, sems.at[6]),
+    ]
+    for t in range(5):
+        for k in range(3):
+            widened[t, :, k * 128 : (k + 1) * 128] = summed[3 * t + k].astype(f32)
+        copies.append(pltpu.make_async_copy(widened.at[t], conv.at[t], sems.at[t]))
+        copies[-1].start()
+    for copy in copies[:2]:
+        copy.start()
+    rows = jnp.concatenate([small[0], small[1]], axis=0).astype(f32)
     for k in range(3):
-        conv[0, :, k * 128 : (k + 1) * 128] = summed[3 * t + k].astype(f32)
-
-    @pl.when(t == 0)
-    def _():
-        rows = jnp.concatenate([small[0], small[1]], axis=0).astype(f32)
-        for k in range(3):
-            for tap in range(15):
-                stem[tap, :, k * 128 : (k + 1) * 128] = rows[k * 64 + 4 * tap : k * 64 + 4 * tap + 4]
-
-
-def finish(summed, small):
+        for tap in range(15):
+            stem[tap, :, k * 128 : (k + 1) * 128] = rows[k * 64 + 4 * tap : k * 64 + 4 * tap + 4]
+    for copy in copies:
+        copy.wait()
+
+
+def finish(summed, small, features, d_pooled):
     vmem = pl.BlockSpec(memory_space=pltpu.VMEM)
+    apart = pl.BlockSpec(memory_space=pl.ANY)
     return pl.pallas_call(
         finish_kernel,
-        grid=(5,),
         out_shape=(
             jax.ShapeDtypeStruct((5, C, C), f32),
             jax.ShapeDtypeStruct((15, 4, C), f32),
+            jax.ShapeDtypeStruct((ROWS, C), bf16),
+            jax.ShapeDtypeStruct((ROWS, C), bf16),
         ),
-        in_specs=[vmem, vmem],
-        out_specs=(
-            pl.BlockSpec((1, C, C), lambda t: (t, 0, 0)),
-            pl.BlockSpec((15, 4, C), lambda t: (0, 0, 0)),
-        ),
+        in_specs=[vmem] * 4,
+        out_specs=(apart, vmem, apart, apart),
+        scratch_shapes=[pltpu.VMEM((5, C, C), f32), pltpu.SemaphoreType.DMA((7,))],
+        compiler_params=pltpu.CompilerParams(vmem_limit_bytes=8 * 1024 * 1024),
         name="finish",
-    )(summed.reshape(16, C, 128), small)
+    )(summed.reshape(16, C, 128), small, features, d_pooled)
 
 
 def per_device(ring, deep, high, codes, variant_pos, variant_shift, stem_weight, conv_weight, cotangent):
     codes = codes.reshape(8, 128)
     cot = cotangent.reshape(ROWS, C)
+    codes, cot, variant_pos, variant_shift, stem_weight, conv_weight = (
+        pltpu.with_memory_space_constraint(array, pltpu.HBM)
+        for array in (codes, cot, variant_pos, variant_shift, stem_weight, conv_weight)
+    )
     near_codes, near_cot = halo(2 * (ring // high) * deep, codes, cot)
     features, d_pooled, summed, small = main(
         ring, deep, high, variant_pos, variant_shift, codes, near_codes, cot, near_cot, stem_weight, conv_weight
     )
-    conv_grad, stem_grad = finish(summed, small)
+    conv_grad, stem_grad, features, d_pooled = finish(summed, small, features, d_pooled)
     return features[None], d_pooled[None], conv_grad, stem_grad
 
 

time: 76 us -> 69.2 us (0.911)
  Pallas kernels: 73.7 us -> 68.4 us
  local copies, waits for them, and re-layouts: 1.5 us -> 0 us
    pallas_call x1, Pallas kernels: 55.2 us -> 52.8 us  [main(): pl.pallas_call(functools.partial(main_kernel, ring, deep, high, count), o...]
    pallas_call x1, Pallas kernels: 4.09 us -> 2.59 us  [finish(): pl.pallas_call(finish_kernel, out_shape=(jax.ShapeDtypeStruct((5, C, C),...]
    unnamed x6 -> x0, local copies, waits for them, and re-layouts: 1.5 us -> none
    pallas_call x1, Pallas kernels: 14.4 us -> 13 us  [halo(): pl.pallas_call(functools.partial(halo_kernel, count), out_shape=(jax.Shap...]
where the time goes in v3:
time: 69.2 us; the launch traced here: 69 us
  Pallas kernels  68.4 us (99%)
    pallas_call x1, Pallas kernels, main(): pl.pallas_call(functools.partial(main_kernel, ring, deep, high, count), o...  52.8 us
    pallas_call x1, Pallas kernels, halo(): pl.pallas_call(functools.partial(halo_kernel, count), out_shape=(jax.Shap...  13 us
    pallas_call x1, Pallas kernels, finish(): pl.pallas_call(finish_kernel, out_shape=(jax.ShapeDtypeStruct((5, C, C),...  2.59 us

profile of v3, /device:TPU:1, one launch (start us, length us, event | category | flops | bytes accessed | tf_op | source)
XLA Modules:
  0.0 69.0 jit_solution(12428373462324076564)
XLA Ops:
  0.6 13.0 %halo.1 = (s32[2,8,128]{2,1,0:T(8,128)S(1)}, bf16[2,16,384]{2,1,0:T(8,128)(2,1)S(1)}) custom-call(s32[8,128]{1,0:T(8,128)} %bitcast.8, bf16[512,384]{1,0:T(8,128)(2,1)} %bitcast.6), custom_call_target="tpu_custom_call" | custom-call | tf_op jit(solution)/shard_map/halo/pallas_call | solution.py:67
  13.7 52.8 %block.1 = (bf16[512,384]{1,0:T(8,128)(2,1)S(1)}, bf16[512,384]{1,0:T(8,128)(2,1)S(1)}, bf16[2,2,4,4,96,128]{5,4,3,2,1,0:T(8,128)(2,1)S(1)}, bf16[2,96,128]{2,1,0:T(8,128)(2,1)S(1)}) custom-call(s32[1,64]{1,0:T(1,128)} %vpos_in.1, s32[1,64]{1,0:T(1,128)} %vshift_in.1, s32[8,128]{1,0:T(8,128)} %bitcast.9, s32[2,8,128]{2,1,0:T(8,128)S(1)} %get-tuple-element.14.near_codes, ...), custom_call_target="tpu_custom_call" | custom-call | tf_op jit(solution)/shard_map/block/pallas_call | solution.py:456
  66.4 2.6 %finish.1 = (f32[5,384,384]{2,1,0:T(8,128)}, f32[15,4,384]{2,1,0:T(4,128)}, bf16[512,384]{1,0:T(8,128)(2,1)}, bf16[512,384]{1,0:T(8,128)(2,1)}) custom-call(bf16[16,384,128]{2,1,0:T(8,128)(2,1)S(1)} %bitcast.5, bf16[2,96,128]{2,1,0:T(8,128)(2,1)S(1)} %get-tuple-element.17.small, bf16[512,384]{1,0:T(8,128)(2,1)S(1)} %get-tuple-element.18.features, ...), custom_call_target="tpu_custom_call" | custom-call | tf_op jit(solution)/shard_map/finish/pallas_call | solution.py:542

commit v4 on v3

--- a/solution.py
+++ b/solution.py
@@ -86,11 +86,11 @@
     features, d_pooled, gathered, stem_all,
     vpos, vshift, codes, cot, stem_weight, insem,
     wt, wf, wsem, ws, stem, slopes, cotx, gx, pooled, pslope, shifted, spread, wins_t, gated_t, dstem,
-    own, s0, r0, s1, r1, a2, s2, r2,
+    own, s0, r0, s1, r1, s2, r2,
     t0, u0, tsum, t1, u1, t2, u2,
-    v3, s3, r3, g3, w3,
+    v3, s3, r3, g3, w3, v4, s4, r4, g4, w4,
     c0s, c0r, c1s, c1r, c2s, c2r, c3s, c3r, d3s, d3r, d2s, d2r, d1s, d1r, d0s, d0r,
-    e0s, e0r, e1s, e1r, e2s, e2r, h0s, h0r,
+    e0s, e0r, e1s, e1r, e2s, e2r, h0s, h0r, c4s, c4r, d4s, d4r,
 ):
     x, y, z, core, device = places(ring, deep, high)
     ctx = lax.axis_index("context")
@@ -232,12 +232,14 @@
         at = pl.multiple_of(owner * 1024 + 256 * j, 256)
         return jnp.dot(gated_t[...], shifted[:, pl.ds(at, 256)], preferred_element_type=f32)
 
+    parts = C // rows2
     for j in range(4):
         block = product(other, j)
         for k in range(2):
             half, sub = divmod(2 * j + k, 4)
             piece, sub = divmod(sub, per)
-            s0[half, piece, sub * C : (sub + 1) * C] = block[:, 128 * k : 128 * (k + 1)].astype(bf16)
+            some = block[:, 128 * k : 128 * (k + 1)].reshape(parts, rows2, 128)
+            s0[half, piece, sub * parts : (sub + 1) * parts] = some.astype(bf16)
             if sub == per - 1:
                 level0(half, piece).start()
     for j in range(4):
@@ -245,22 +247,30 @@
         for k in range(2):
             half, sub = divmod(2 * j + k, 4)
             piece, sub = divmod(sub, per)
-            own[half, piece, sub * C : (sub + 1) * C] = block[:, 128 * k : 128 * (k + 1)]
-
-    def level1(half, step):
+            some = block[:, 128 * k : 128 * (k + 1)].reshape(parts, rows2, 128)
+            own[half, piece, sub * parts : (sub + 1) * parts] = some
+
+    def ahead(half, level, step):
+        return lax.rem(mine(half, level) + step, ring)
+
+    def behind(half, level, step):
+        return lax.rem(mine(half, level) + ring - step, ring)
+
+    def level1(half, step, chunk):
         return remote(
-            s1.at[half, step - 1], r1.at[half, step - 1], c1s.at[half, step - 1], c1r.at[half, step - 1],
-            along(half, 1, step),
+            s1.at[half, step - 1, chunk], r1.at[half, step - 1, chunk],
+            c1s.at[half, step - 1, chunk], c1r.at[half, step - 1, chunk], along(half, 1, step),
         )
 
     for half in range(2):
         for piece in range(ring):
             level0(half, piece).wait_recv()
-    for step in order:
-        for half in range(2):
-            piece = lax.rem(mine(half, 1) + step, ring)
-            s1[half, step - 1] = (own[half, piece] + r0[half, piece].astype(f32)).astype(bf16)
-            level1(half, step).start()
+    for chunk in order + [0]:
+        for step in order:
+            for half in range(2):
+                at = ahead(half, 1, step), ahead(half, 2, chunk)
+                s1[half, step - 1, chunk] = (own[half, at[0], at[1]] + r0[half, at[0], at[1]].astype(f32)).astype(bf16)
+                level1(half, step, chunk).start()
 
     for load in loads:
         load.wait()
@@ -309,21 +319,22 @@
 
     def level2(half, step):
         return remote(
-            s2.at[half, lax.rem(mine(half, 2) + step, ring)], r2.at[half, step - 1],
-            c2s.at[half, step - 1], c2r.at[half, step - 1], along(half, 2, step),
+            s2.at[half, step - 1], r2.at[half, step - 1], c2s.at[half, step - 1], c2r.at[half, step - 1],
+            along(half, 2, step),
         )
 
-    for half in range(2):
-        piece = mine(half, 1)
-        total = own[half, piece] + r0[half, piece].astype(f32)
-        for step in range(1, ring):
-            level1(half, step).wait_recv()
-            total = total + r1[half, step - 1].astype(f32)
-        total = total.reshape(a2.shape[1:])
-        a2[half] = total
-        s2[half] = total.astype(bf16)
-        for step in order:
-            level2(half, step).start()
+    for chunk in order + [0]:
+        for half in range(2):
+            at = mine(half, 1), ahead(half, 2, chunk)
+            total = own[half, at[0], at[1]] + r0[half, at[0], at[1]].astype(f32)
+            for step in range(1, ring):
+                level1(half, step, chunk).wait_recv()
+                total = total + r1[half, step - 1, chunk].astype(f32)
+            if chunk:
+                s2[half, chunk - 1] = total.astype(bf16)
+                level2(half, chunk).start()
+            else:
+                v3[half * rows2 : (half + 1) * rows2] = total
 
     for step in range(1, ring):
         stem1(step).wait_recv()
@@ -332,121 +343,132 @@
     for step in order:
         stem2(step).start()
 
+    def far(i):
+        half_way = deep // 2 - lax.div(i + 1, 2)
+        return jnp.where(lax.rem(i, 2) == 0, half_way, deep - half_way)
+
+    def down(send, land, sends, recvs):
+        return lambda step: remote(
+            send.at[lax.rem(z + step, deep)], land.at[step - 1], sends.at[step - 1], recvs.at[step - 1], deeper(step)
+        )
+
+    def up(all_of, sends, recvs):
+        return lambda step: remote(all_of.at[z], all_of.at[z], sends.at[step - 1], recvs.at[step - 1], deeper(step))
+
+    def start_all(copy):
+        def one(i, carry):
+            copy(far(i)).start()
+            return carry
+
+        lax.fori_loop(0, deep - 1, one, 0)
+
+    def each(method, *copies):
+        def one(i, carry):
+            for copy in copies:
+                getattr(copy(i + 1), method)()
+            return carry
+
+        lax.fori_loop(0, deep - 1, one, 0)
+
+    def cut(source, send, share):
+        for piece in range(deep):
+            send[piece] = source[piece * share : piece * share + send.shape[1]].astype(bf16)
+
+    def join(all_of, target, share):
+        for piece in range(deep):
+            target[piece * share : piece * share + all_of.shape[1]] = all_of[piece].astype(f32)
+
+    def summed(copy, send, land):
+        def one(i, total):
+            copy(i + 1).wait_recv()
+            return total + land[i].astype(f32)
+
+        return lax.fori_loop(0, deep - 1, one, send[z].astype(f32)).astype(bf16)
+
     for half in range(2):
-        total = a2[half, mine(half, 2)]
-        for step in range(1, ring):
+        total = v3[half * rows2 : (half + 1) * rows2]
+        for step in near:
             level2(half, step).wait_recv()
             total = total + r2[half, step - 1].astype(f32)
         v3[half * rows2 : (half + 1) * rows2] = total
+    conv_down, conv_up = down(s3, r3, c3s, c3r), up(g3, d3s, d3r)
+    stem_down, stem_up = down(s4, r4, c4s, c4r), up(g4, d4s, d4r)
+    cut(v3, s3, 2 * rows2 // deep)
+    start_all(conv_down)
     for step in range(1, ring):
         stem2(step).wait_recv()
         small = small + u2[step - 1].astype(f32)
-    v3[2 * rows2 : 2 * rows2 + 96] = small
-    share = (2 * rows2 + 96) // deep
-    tall = s3.shape[1]
-    for piece in range(deep):
-        s3[piece] = v3[piece * share : piece * share + tall].astype(bf16)
-
-    def level3(step):
-        return remote(
-            s3.at[lax.rem(z + step, deep)], r3.at[step - 1], c3s.at[step - 1], c3r.at[step - 1], deeper(step)
-        )
-
-    def back3(step):
-        return remote(g3.at[z], g3.at[z], d3s.at[step - 1], d3r.at[step - 1], deeper(step))
-
-    def far(i):
-        half_way = deep // 2 - lax.div(i + 1, 2)
-        return jnp.where(lax.rem(i, 2) == 0, half_way, deep - half_way)
-
-    def send3(i, carry):
-        level3(far(i)).start()
-        return carry
-
-    lax.fori_loop(0, deep - 1, send3, 0)
-
-    def take3(i, total):
-        level3(i + 1).wait_recv()
-        return total + r3[i].astype(f32)
-
-    g3[z] = lax.fori_loop(0, deep - 1, take3, s3[z].astype(f32)).astype(bf16)
-
-    def spread3(i, carry):
-        back3(far(i)).start()
-        return carry
-
-    lax.fori_loop(0, deep - 1, spread3, 0)
-
-    def got3(i, carry):
-        back3(i + 1).wait_recv()
-        return carry
-
-    lax.fori_loop(0, deep - 1, got3, 0)
-    for piece in range(deep):
-        w3[piece * share : piece * share + tall] = g3[piece].astype(f32)
+    v4[0:96] = small
+    cut(v4, s4, 96 // deep)
+    start_all(stem_down)
+    g3[z] = summed(conv_down, s3, r3)
+    start_all(conv_up)
+    g4[z] = summed(stem_down, s4, r4)
+    start_all(stem_up)
+    each("wait_recv", conv_up)
+    join(g3, w3, 2 * rows2 // deep)
 
     def back2(half, step):
         spot = gathered.at[core, half, mine(half, 1), mine(half, 2)]
         return remote(spot, spot, d2s.at[half, step - 1], d2r.at[half, step - 1], along(half, 2, step))
+
+    def back1(half, step, chunk):
+        spot = gathered.at[core, half, mine(half, 1), behind(half, 2, chunk)]
+        return remote(spot, spot, d1s.at[half, step - 1, chunk], d1r.at[half, step - 1, chunk], along(half, 1, step))
+
+    def back0(half, step, chunk):
+        spot = gathered.at[core, half, behind(half, 1, step), behind(half, 2, chunk)]
+        return remote(spot, spot, d0s.at[half, step, chunk], d0r.at[half, step, chunk], sibling)
 
     for half in range(2):
         gathered[core, half, mine(half, 1), mine(half, 2)] = w3[half * rows2 : (half + 1) * rows2].astype(bf16)
         for step in order:
             back2(half, step).start()
+    for chunk in [0] + near:
+        for half in range(2):
+            if chunk:
+                back2(half, chunk).wait_recv()
+            for step in order:
+                back1(half, step, chunk).start()
+            back0(half, 0, chunk).start()
+
+    each("wait_recv", stem_up)
+    join(g4, w4, 96 // deep)
 
     def back_stem():
         return remote(stem_all.at[core], stem_all.at[core], h0s, h0r, sibling)
 
-    stem_all[core] = w3[2 * rows2 : 2 * rows2 + 96].astype(bf16)
+    stem_all[core] = w4[0:96].astype(bf16)
     back_stem().start()
-
-    def back1(half, step):
-        spot = gathered.at[core, half, mine(half, 1)]
-        return remote(spot, spot, d1s.at[half, step - 1], d1r.at[half, step - 1], along(half, 1, step))
-
-    def back0(half, step):
-        spot = gathered.at[core, half, lax.rem(mine(half, 1) + ring - step, ring)]
-        return remote(spot, spot, d0s.at[half, step], d0r.at[half, step], sibling)
-
-    for half in range(2):
-        for step in range(1, ring):
-            back2(half, step).wait_recv()
-        for step in order:
-            back1(half, step).start()
-        back0(half, 0).start()
-    for step in near:
-        for half in range(2):
-            back1(half, step).wait_recv()
-            back0(half, step).start()
+    for chunk in [0] + near:
+        for step in near:
+            for half in range(2):
+                back1(half, step, chunk).wait_recv()
+                back0(half, step, chunk).start()
     back_stem().wait()
     stem0().wait_send()
     for half in range(2):
         for step in range(ring):
-            back0(half, step).wait()
             level0(half, step).wait_send()
+            for chunk in range(ring):
+                back0(half, step, chunk).wait()
         for step in range(1, ring):
-            level1(half, step).wait_send()
             level2(half, step).wait_send()
             back2(half, step).wait_send()
-            back1(half, step).wait_send()
+            for chunk in range(ring):
+                level1(half, step, chunk).wait_send()
+                back1(half, step, chunk).wait_send()
     for step in range(1, ring):
         stem1(step).wait_send()
         stem2(step).wait_send()
-
-    def sent3(i, carry):
-        level3(i + 1).wait_send()
-        back3(i + 1).wait_send()
-        return carry
-
-    lax.fori_loop(0, deep - 1, sent3, 0)
+    each("wait_send", conv_down, conv_up, stem_down, stem_up)
 
 
 def main(ring, deep, high, vpos, vshift, codes, near_codes, cot, near_cot, stem_weight, weight):
     per = 4 // ring
     rows1 = per * C
     rows2 = rows1 // ring
-    share = (2 * rows2 + 96) // deep
-    tall = -(-share // 8) * 8
+    talls = [-(-total // (8 * deep)) * 8 for total in (2 * rows2, 96)]
     count = 2 * (ring // high) * deep
     dma = pltpu.SemaphoreType.DMA
     halves = lambda *lead: pltpu.VMEM((2,) + lead, bf16)
@@ -485,13 +507,12 @@
             pltpu.VMEM((64, ROWS), bf16),
             pltpu.VMEM((C, ROWS), bf16),
             pltpu.VMEM((ROWS, 2 * C), bf16),
-            pltpu.VMEM((2, ring, rows1, 128), f32),
-            halves(ring, rows1, 128),
-            halves(ring, rows1, 128),
-            halves(ring - 1, rows1, 128),
-            halves(ring - 1, rows1, 128),
-            pltpu.VMEM((2, ring, rows2, 128), f32),
-            halves(ring, rows2, 128),
+            pltpu.VMEM((2, ring, ring, rows2, 128), f32),
+            halves(ring, ring, rows2, 128),
+            halves(ring, ring, rows2, 128),
+            halves(ring - 1, ring, rows2, 128),
+            halves(ring - 1, ring, rows2, 128),
+            halves(ring - 1, rows2, 128),
             halves(ring - 1, rows2, 128),
             pltpu.VMEM((96, 128), bf16),
             pltpu.VMEM((96, 128), bf16),
@@ -500,14 +521,21 @@
             pltpu.VMEM((ring - 1, 96, 128), bf16),
             pltpu.VMEM((96, 128), bf16),
             pltpu.VMEM((ring - 1, 96, 128), bf16),
-            pltpu.VMEM((2 * rows2 + 96 + tall, 128), f32),
-            pltpu.VMEM((deep, tall, 128), bf16),
-            pltpu.VMEM((deep - 1, tall, 128), bf16),
-            pltpu.VMEM((deep, tall, 128), bf16),
-            pltpu.VMEM((2 * rows2 + 96 + tall, 128), f32),
-            *pair(2, ring), *pair(2, ring - 1), *pair(2, ring - 1), *pair(deep - 1),
-            *pair(deep - 1), *pair(2, ring - 1), *pair(2, ring - 1), *pair(2, ring),
+            *[
+                scratch
+                for tall, total in zip(talls, (2 * rows2, 96))
+                for scratch in (
+                    pltpu.VMEM((total + tall, 128), f32),
+                    pltpu.VMEM((deep, tall, 128), bf16),
+                    pltpu.VMEM((deep - 1, tall, 128), bf16),
+                    pltpu.VMEM((deep, tall, 128), bf16),
+                    pltpu.VMEM((total + tall, 128), f32),
+                )
+            ],
+            *pair(2, ring), *pair(2, ring - 1, ring), *pair(2, ring - 1), *pair(deep - 1),
+            *pair(deep - 1), *pair(2, ring - 1), *pair(2, ring - 1, ring), *pair(2, ring, ring),
             *pair(), *pair(ring - 1), *pair(ring - 1), *pair(),
+            *pair(deep - 1), *pair(deep - 1),
         ],
         compiler_params=pltpu.CompilerParams(
             collective_id=1, has_side_effects=True, vmem_limit_bytes=36 * 1024 * 1024

time: 69.2 us -> 66.1 us (0.955)
  Pallas kernels: 68.4 us -> 65.3 us
    pallas_call x1, Pallas kernels: 52.8 us -> 49.7 us  [main(): pl.pallas_call(functools.partial(main_kernel, ring, deep, high, count), o...]
where the time goes in v4:
time: 66.1 us; the launch traced here: 65.9 us
  Pallas kernels  65.3 us (99%)
    pallas_call x1, Pallas kernels, main(): pl.pallas_call(functools.partial(main_kernel, ring, deep, high, count), o...  49.7 us
    pallas_call x1, Pallas kernels, halo(): pl.pallas_call(functools.partial(halo_kernel, count), out_shape=(jax.Shap...  13 us
    pallas_call x1, Pallas kernels, finish(): pl.pallas_call(finish_kernel, out_shape=(jax.ShapeDtypeStruct((5, C, C),...  2.59 us

profile of v4, /device:TPU:1, one launch (start us, length us, event | category | flops | bytes accessed | tf_op | source)
XLA Modules:
  0.0 65.9 jit_solution(4883474886979160351)
XLA Ops:
  0.6 13.0 %halo.1 = (s32[2,8,128]{2,1,0:T(8,128)S(1)}, bf16[2,16,384]{2,1,0:T(8,128)(2,1)S(1)}) custom-call(s32[8,128]{1,0:T(8,128)} %bitcast.8, bf16[512,384]{1,0:T(8,128)(2,1)} %bitcast.6), custom_call_target="tpu_custom_call" | custom-call | tf_op jit(solution)/shard_map/halo/pallas_call | solution.py:67
  13.7 49.7 %block.1 = (bf16[512,384]{1,0:T(8,128)(2,1)S(1)}, bf16[512,384]{1,0:T(8,128)(2,1)S(1)}, bf16[2,2,4,4,96,128]{5,4,3,2,1,0:T(8,128)(2,1)S(1)}, bf16[2,96,128]{2,1,0:T(8,128)(2,1)S(1)}) custom-call(s32[1,64]{1,0:T(1,128)} %vpos_in.1, s32[1,64]{1,0:T(1,128)} %vshift_in.1, s32[8,128]{1,0:T(8,128)} %bitcast.9, s32[2,8,128]{2,1,0:T(8,128)S(1)} %get-tuple-element.14.near_codes, ...), custom_call_target="tpu_custom_call" | custom-call | tf_op jit(solution)/shard_map/block/pallas_call | solution.py:478
  63.4 2.6 %finish.1 = (f32[5,384,384]{2,1,0:T(8,128)}, f32[15,4,384]{2,1,0:T(4,128)}, bf16[512,384]{1,0:T(8,128)(2,1)}, bf16[512,384]{1,0:T(8,128)(2,1)}) custom-call(bf16[16,384,128]{2,1,0:T(8,128)(2,1)S(1)} %bitcast.5, bf16[2,96,128]{2,1,0:T(8,128)(2,1)S(1)} %get-tuple-element.17.small, bf16[512,384]{1,0:T(8,128)(2,1)S(1)} %get-tuple-element.18.features, ...), custom_call_target="tpu_custom_call" | custom-call | tf_op jit(solution)/shard_map/finish/pallas_call | solution.py:570

commit v5 on v4

--- a/solution.py
+++ b/solution.py
@@ -43,48 +43,11 @@
     )
 
 
-def halo_kernel(count, codes, cot, near_codes, near_cot, sends, recvs):
-    ctx = lax.axis_index("context")
-    left = {"context": lax.rem(ctx + count - 1, count)}
-    right = {"context": lax.rem(ctx + 1, count)}
-    barrier = pltpu.get_barrier_semaphore()
-    for to in (left, right):
-        pl.semaphore_signal(barrier, inc=1, device_id=to, device_id_type=MESH)
-    pl.semaphore_wait(barrier, 2)
-    copies = [
-        remote(codes, near_codes.at[0], sends.at[0], recvs.at[0], right),
-        remote(codes, near_codes.at[1], sends.at[1], recvs.at[1], left),
-        remote(cot.at[ROWS - LEAD : ROWS], near_cot.at[0], sends.at[2], recvs.at[2], right),
-        remote(cot.at[0:LEAD], near_cot.at[1], sends.at[3], recvs.at[3], left),
-    ]
-    for copy in copies:
-        copy.start()
-    for copy in copies:
-        copy.wait()
-
-
-def halo(count, codes, cot):
-    return pl.pallas_call(
-        functools.partial(halo_kernel, count),
-        out_shape=(
-            jax.ShapeDtypeStruct((2, 8, 128), jnp.int32),
-            jax.ShapeDtypeStruct((2, LEAD, C), bf16),
-        ),
-        in_specs=[pl.BlockSpec(memory_space=pltpu.HBM)] * 2,
-        out_specs=(pl.BlockSpec(memory_space=pltpu.VMEM),) * 2,
-        scratch_shapes=[pltpu.SemaphoreType.DMA((4,)), pltpu.SemaphoreType.DMA((4,))],
-        compiler_params=pltpu.CompilerParams(
-            collective_id=0, has_side_effects=True, vmem_limit_bytes=2 * 1024 * 1024
-        ),
-        name="halo",
-    )(codes, cot)
-
-
 def main_kernel(
     ring, deep, high, count,
-    vpos_in, vshift_in, codes_in, near_codes, cot_in, near_cot, stem_weight_in, weight,
+    vpos_in, vshift_in, codes_in, cot_in, stem_weight_in, weight,
     features, d_pooled, gathered, stem_all,
-    vpos, vshift, codes, cot, stem_weight, insem,
+    vpos, vshift, codes, cot, stem_weight, insem, near_codes, near_cot, hs, hr, known, wcat,
     wt, wf, wsem, ws, stem, slopes, cotx, gx, pooled, pslope, shifted, spread, wins_t, gated_t, dstem,
     own, s0, r0, s1, r1, s2, r2,
     t0, u0, tsum, t1, u1, t2, u2,
@@ -122,35 +85,79 @@
     ]
     for feed in feeds:
         feed.start()
-    barrier = pltpu.get_barrier_semaphore()
-    pl.semaphore_signal(barrier, inc=1, device_id=sibling, device_id_type=MESH)
-
-    def greet(step, carry):
-        pl.semaphore_signal(barrier, inc=1, device_id=deeper(step), device_id_type=MESH)
-        return carry
-
-    lax.fori_loop(1, deep, greet, 0)
-    for step in range(1, ring):
-        for half in range(2):
-            pl.semaphore_signal(barrier, inc=1, device_id=along(half, 1, step), device_id_type=MESH)
-
     loads = [pltpu.make_async_copy(weight.at[t], wt.at[:, t * C : (t + 1) * C], wsem.at[t]) for t in range(5)]
     loads += [pltpu.make_async_copy(weight.at[t], wf.at[t * C : (t + 1) * C], wsem.at[5 + t]) for t in range(5)]
     for load in loads:
         load.start()
 
-    for feed in feeds[:3]:
-        feed.wait()
-    bases = jnp.concatenate(
-        [near_codes[0, 7:8], codes[...], near_codes[1, 0:1], jnp.zeros((6, 128), jnp.int32)], axis=0
-    )
+    left = {"context": lax.rem(ctx + count - 1, count)}
+    right = {"context": lax.rem(ctx + 1, count)}
+    barrier = pltpu.get_barrier_semaphore()
+    greeted = [left, right, deeper(1), deeper(deep - 1)]
+    greeted += [along(half, 1, step) for step in range(1, ring) for half in range(2)]
+    for to in greeted:
+        pl.semaphore_signal(barrier, inc=1, device_id=to, device_id_type=MESH)
+
+    ws[...] = jnp.zeros_like(ws)
+    feeds[3].wait()
+    for k in range(15):
+        ws[4 * k : 4 * k + 4, 0:C] = stem_weight[k]
+        ws[4 * k + 4 : 4 * k + 8, C:] = stem_weight[k]
+    taps = ws[...]
+    upper = taps.astype(bf16)
+    wcat[0:64] = upper
+    wcat[64:128] = (taps - upper.astype(f32)).astype(bf16)
+    for i in (0, 1, 2, 4):
+        feeds[i].wait()
+
+    pl.semaphore_wait(barrier, len(greeted))
+    halos = [
+        remote(codes, near_codes.at[0], hs.at[0], hr.at[0], right),
+        remote(codes, near_codes.at[1], hs.at[1], hr.at[1], left),
+        remote(cot.at[ROWS - LEAD : ROWS], near_cot.at[0], hs.at[2], hr.at[2], right),
+        remote(cot.at[0:LEAD], near_cot.at[1], hs.at[3], hr.at[3], left),
+    ]
+    for copy in halos:
+        copy.start()
+    reach = [1 << m for m in range(8) if (1 << m) < deep // 2]
+
+    def tell(m):
+        for step in (reach[m], deep - reach[m]):
+            pl.semaphore_signal(known.at[m], inc=1, device_id=deeper(step), device_id_type=MESH)
+
+    def learn(m):
+        if m < len(reach):
+            pl.semaphore_wait(known.at[m], 2)
+            if m + 1 < len(reach):
+                tell(m + 1)
+
+    if reach:
+        tell(0)
+
+    cotx[LEAD : LEAD + ROWS] = cot[...].astype(f32)
+
+    def shift_in(first, size):
+        for t in range(5):
+            at = LEAD + 2 - t + first
+            shifted[first : first + size, t * C : (t + 1) * C] = cotx[at : at + size].astype(bf16)
+
+    shift_in(LEAD, ROWS - 2 * LEAD)
+    shifted[:, 5 * C :] = jnp.zeros((ROWS, 128), bf16)
     spot = (
         ctx * (2 * ROWS) - 128
         + 128 * lax.broadcasted_iota(jnp.int32, (16, 128), 0)
         + lax.broadcasted_iota(jnp.int32, (16, 128), 1)
     )
+    moved = jnp.zeros((16, 128), jnp.int32)
     for v in range(vpos.shape[1]):
-        bases = bases + jnp.where(spot == vpos[0, v], vshift[0, v], 0)
+        moved = moved + jnp.where(spot == vpos[0, v], vshift[0, v], 0)
+
+    for copy in halos:
+        copy.wait_recv()
+    learn(0)
+    bases = moved + jnp.concatenate(
+        [near_codes[0, 7:8], codes[...], near_codes[1, 0:1], jnp.zeros((6, 128), jnp.int32)], axis=0
+    )
     bases = jnp.where((spot >= 0) & (spot < count * (2 * ROWS)), bases & 3, 4)
     lane_in = lax.broadcasted_iota(jnp.int32, (128, 128), 0)
     lane_out = lax.broadcasted_iota(jnp.int32, (128, 128), 1)
@@ -175,15 +182,7 @@
     )
     wins_t[...] = kept.astype(bf16)
 
-    feeds[3].wait()
-    ws[...] = jnp.zeros_like(ws)
-    for k in range(15):
-        ws[4 * k : 4 * k + 4, 0:C] = stem_weight[k]
-        ws[4 * k + 4 : 4 * k + 8, C:] = stem_weight[k]
-    taps = ws[...]
-    upper = taps.astype(bf16)
-    lower = (taps - upper.astype(f32)).astype(bf16)
-    stem[...] = jnp.dot(windows, jnp.concatenate([upper, lower], axis=0), preferred_element_type=f32)
+    stem[...] = jnp.dot(windows, wcat[...], preferred_element_type=f32)
 
     def bend(value):
         square = value * value
@@ -214,14 +213,9 @@
     gx[LEAD + ROWS :] = gx[LEAD + ROWS :] * inside_right
     cotx[0:LEAD] = near_cot[0].astype(f32) * inside_left
     cotx[LEAD + ROWS :] = near_cot[1].astype(f32) * inside_right
-    feeds[4].wait()
-    cotx[LEAD : LEAD + ROWS] = cot[...].astype(f32)
+    shift_in(0, LEAD)
+    shift_in(ROWS - LEAD, LEAD)
     gated_t[...] = gx[LEAD : LEAD + ROWS].T.astype(bf16)
-    for t in range(5):
-        shifted[:, t * C : (t + 1) * C] = cotx[LEAD + 2 - t : LEAD + 2 - t + ROWS].astype(bf16)
-    shifted[:, 5 * C :] = jnp.zeros((ROWS, 128), bf16)
-
-    pl.semaphore_wait(barrier, 1 + 2 * (ring - 1) + deep - 1)
 
     def level0(half, piece):
         return remote(
@@ -272,6 +266,7 @@
                 s1[half, step - 1, chunk] = (own[half, at[0], at[1]] + r0[half, at[0], at[1]].astype(f32)).astype(bf16)
                 level1(half, step, chunk).start()
 
+    learn(1)
     for load in loads:
         load.wait()
     for block in range(2):
@@ -393,6 +388,8 @@
         v3[half * rows2 : (half + 1) * rows2] = total
     conv_down, conv_up = down(s3, r3, c3s, c3r), up(g3, d3s, d3r)
     stem_down, stem_up = down(s4, r4, c4s, c4r), up(g4, d4s, d4r)
+    for m in range(2, len(reach)):
+        learn(m)
     cut(v3, s3, 2 * rows2 // deep)
     start_all(conv_down)
     for step in range(1, ring):
@@ -446,6 +443,8 @@
                 back1(half, step, chunk).wait_recv()
                 back0(half, step, chunk).start()
     back_stem().wait()
+    for copy in halos:
+        copy.wait_send()
     stem0().wait_send()
     for half in range(2):
         for step in range(ring):
@@ -464,7 +463,7 @@
     each("wait_send", conv_down, conv_up, stem_down, stem_up)
 
 
-def main(ring, deep, high, vpos, vshift, codes, near_codes, cot, near_cot, stem_weight, weight):
+def main(ring, deep, high, vpos, vshift, codes, cot, stem_weight, weight):
     per = 4 // ring
     rows1 = per * C
     rows2 = rows1 // ring
@@ -483,7 +482,7 @@
             jax.ShapeDtypeStruct((2, 2, ring, ring, rows2, 128), bf16),
             jax.ShapeDtypeStruct((2, 96, 128), bf16),
         ),
-        in_specs=[hbm, hbm, hbm, vmem, hbm, vmem, hbm, hbm],
+        in_specs=[hbm] * 6,
         out_specs=(vmem,) * 4,
         scratch_shapes=[
             pltpu.SMEM(vpos.shape, jnp.int32),
@@ -492,6 +491,11 @@
             pltpu.VMEM((ROWS, C), bf16),
             pltpu.VMEM((15, 4, C), f32),
             dma((5,)),
+            pltpu.VMEM((2, 8, 128), jnp.int32),
+            pltpu.VMEM((2, LEAD, C), bf16),
+            *pair(4),
+            pltpu.SemaphoreType.REGULAR((3,)),
+            pltpu.VMEM((128, 2 * C), bf16),
             pltpu.VMEM((C, 5 * C), bf16),
             pltpu.VMEM((5 * C, C), bf16),
             dma((10,)),
@@ -538,10 +542,10 @@
             *pair(deep - 1), *pair(deep - 1),
         ],
         compiler_params=pltpu.CompilerParams(
-            collective_id=1, has_side_effects=True, vmem_limit_bytes=36 * 1024 * 1024
+            collective_id=0, has_side_effects=True, vmem_limit_bytes=36 * 1024 * 1024
         ),
         name="block",
-    )(vpos, vshift, codes, near_codes, cot, near_cot, stem_weight, weight)
+    )(vpos, vshift, codes, cot, stem_weight, weight)
 
 
 def finish_kernel(summed, small, features, d_pooled, conv, stem, features_out, d_pooled_out, widened, sems):
@@ -590,9 +594,8 @@
         pltpu.with_memory_space_constraint(array, pltpu.HBM)
         for array in (codes, cot, variant_pos, variant_shift, stem_weight, conv_weight)
     )
-    near_codes, near_cot = halo(2 * (ring // high) * deep, codes, cot)
     features, d_pooled, summed, small = main(
-        ring, deep, high, variant_pos, variant_shift, codes, near_codes, cot, near_cot, stem_weight, conv_weight
+        ring, deep, high, variant_pos, variant_shift, codes, cot, stem_weight, conv_weight
     )
     conv_grad, stem_grad, features, d_pooled = finish(summed, small, features, d_pooled)
     return features[None], d_pooled[None], conv_grad, stem_grad

time: 66.1 us -> 62.6 us (0.947)
  Pallas kernels: 65.3 us -> 61.8 us
    pallas_call x1 -> x0, Pallas kernels: 13 us -> none  [halo(): pl.pallas_call(functools.partial(halo_kernel, count), out_shape=(jax.Shap...]
    pallas_call x1, Pallas kernels: 49.7 us -> 59.2 us  [main(): pl.pallas_call(functools.partial(main_kernel, ring, deep, high, count), o...]
where the time goes in v5:
time: 62.6 us; the launch traced here: 62.4 us
  Pallas kernels  61.8 us (99%)
  between operations  0.64 us (1%)
    pallas_call x1, Pallas kernels, main(): pl.pallas_call(functools.partial(main_kernel, ring, deep, high, count), o...  59.2 us
    pallas_call x1, Pallas kernels, finish(): pl.pallas_call(finish_kernel, out_shape=(jax.ShapeDtypeStruct((5, C, C),...  2.59 us

profile of v5, /device:TPU:1, one launch (start us, length us, event | category | flops | bytes accessed | tf_op | source)
XLA Modules:
  0.0 62.4 jit_solution(7956635721202947144)
XLA Ops:
  0.6 59.2 %block.1 = (bf16[512,384]{1,0:T(8,128)(2,1)S(1)}, bf16[512,384]{1,0:T(8,128)(2,1)S(1)}, bf16[2,2,4,4,96,128]{5,4,3,2,1,0:T(8,128)(2,1)S(1)}, bf16[2,96,128]{2,1,0:T(8,128)(2,1)S(1)}) custom-call(s32[1,64]{1,0:T(1,128)} %vpos_in.1, s32[1,64]{1,0:T(1,128)} %vshift_in.1, s32[8,128]{1,0:T(8,128)} %bitcast.7, bf16[512,384]{1,0:T(8,128)(2,1)} %bitcast.6, ...), custom_call_target="tpu_custom_call" | custom-call | tf_op jit(solution)/shard_map/block/pallas_call | solution.py:477
  59.8 2.6 %finish.1 = (f32[5,384,384]{2,1,0:T(8,128)}, f32[15,4,384]{2,1,0:T(4,128)}, bf16[512,384]{1,0:T(8,128)(2,1)}, bf16[512,384]{1,0:T(8,128)(2,1)}) custom-call(bf16[16,384,128]{2,1,0:T(8,128)(2,1)S(1)} %bitcast.5, bf16[2,96,128]{2,1,0:T(8,128)(2,1)S(1)} %get-tuple-element.13.small, bf16[512,384]{1,0:T(8,128)(2,1)S(1)} %get-tuple-element.14.features, ...), custom_call_target="tpu_custom_call" | custom-call | tf_op jit(solution)/shard_map/finish/pallas_call | solution.py:574

commit v6 on v5

--- a/solution.py
+++ b/solution.py
@@ -87,9 +87,6 @@
         feed.start()
     loads = [pltpu.make_async_copy(weight.at[t], wt.at[:, t * C : (t + 1) * C], wsem.at[t]) for t in range(5)]
     loads += [pltpu.make_async_copy(weight.at[t], wf.at[t * C : (t + 1) * C], wsem.at[5 + t]) for t in range(5)]
-    for load in loads:
-        load.start()
-
     left = {"context": lax.rem(ctx + count - 1, count)}
     right = {"context": lax.rem(ctx + 1, count)}
     barrier = pltpu.get_barrier_semaphore()
@@ -119,6 +116,8 @@
     ]
     for copy in halos:
         copy.start()
+    for load in loads:
+        load.start()
     reach = [1 << m for m in range(8) if (1 << m) < deep // 2]
 
     def tell(m):
@@ -152,37 +151,30 @@
     for v in range(vpos.shape[1]):
         moved = moved + jnp.where(spot == vpos[0, v], vshift[0, v], 0)
 
-    for copy in halos:
-        copy.wait_recv()
-    learn(0)
-    bases = moved + jnp.concatenate(
-        [near_codes[0, 7:8], codes[...], near_codes[1, 0:1], jnp.zeros((6, 128), jnp.int32)], axis=0
-    )
-    bases = jnp.where((spot >= 0) & (spot < count * (2 * ROWS)), bases & 3, 4)
+    inside = (spot >= 0) & (spot < count * (2 * ROWS))
     lane_in = lax.broadcasted_iota(jnp.int32, (128, 128), 0)
     lane_out = lax.broadcasted_iota(jnp.int32, (128, 128), 1)
     pick = (lane_in == 2 * (lane_out & 63) + lax.shift_right_logical(lane_out, 6)).astype(f32).astype(bf16)
-    split = jnp.dot(bases.astype(f32).astype(bf16), pick, preferred_element_type=f32)
-    turned = pltpu.roll(split, 64, 1)
     first = lax.broadcasted_iota(jnp.int32, (1, 128), 1) < 64
-    evens, odds = [], []
-    for p in range(5):
-        evens.append(jnp.where(first, split[2 * p : 2 * p + 1], turned[2 * p + 1 : 2 * p + 2]))
-        odds.append(jnp.where(first, turned[2 * p : 2 * p + 1], split[2 * p + 1 : 2 * p + 2]))
-    even = jnp.broadcast_to(jnp.concatenate(evens, axis=1), (8, LANES))
-    odd = jnp.broadcast_to(jnp.concatenate(odds, axis=1), (8, LANES))
     line = lax.broadcasted_iota(jnp.int32, (8, LANES), 0)
-    both = jnp.where(line < 4, odd, pltpu.roll(even, LANES - 1, 1))
-    hot = (both == (line & 3).astype(f32)).astype(f32)
-    wide = [pltpu.roll(hot, LANES - (PAIRS + q), 1) for q in range(8)]
-    windows_t = jnp.concatenate(wide + wide, axis=0)
-    windows = windows_t.T[:TALL].astype(bf16)
-    kept = jnp.concatenate(
-        [pltpu.roll(hot, LANES - (PAIRS + LEAD + q), 1)[:, :ROWS] for q in range(8)], axis=0
-    )
-    wins_t[...] = kept.astype(bf16)
-
-    stem[...] = jnp.dot(windows, wcat[...], preferred_element_type=f32)
+
+    def one_hot(before, after):
+        bases = moved + jnp.concatenate([before, codes[...], after, jnp.zeros((6, 128), jnp.int32)], axis=0)
+        bases = jnp.where(inside, bases & 3, 4)
+        split = jnp.dot(bases.astype(f32).astype(bf16), pick, preferred_element_type=f32)
+        turned = pltpu.roll(split, 64, 1)
+        evens, odds = [], []
+        for p in range(5):
+            evens.append(jnp.where(first, split[2 * p : 2 * p + 1], turned[2 * p + 1 : 2 * p + 2]))
+            odds.append(jnp.where(first, turned[2 * p : 2 * p + 1], split[2 * p + 1 : 2 * p + 2]))
+        even = jnp.broadcast_to(jnp.concatenate(evens, axis=1), (8, LANES))
+        odd = jnp.broadcast_to(jnp.concatenate(odds, axis=1), (8, LANES))
+        both = jnp.where(line < 4, odd, pltpu.roll(even, LANES - 1, 1))
+        return (both == (line & 3).astype(f32)).astype(f32)
+
+    def windows_of(hot):
+        wide = [pltpu.roll(hot, LANES - (PAIRS + q), 1) for q in range(8)]
+        return jnp.concatenate(wide + wide, axis=0)
 
     def bend(value):
         square = value * value
@@ -206,7 +198,25 @@
         pslope[rows] = slope
         return carry
 
-    lax.fori_loop(0, TALL // 16, activate, 0)
+    edge = 2 * LEAD
+    blank = jnp.zeros((1, 128), jnp.int32)
+    windows = windows_of(one_hot(blank, blank)).T[edge : TALL - edge].astype(bf16)
+    stem[edge : TALL - edge] = jnp.dot(windows, wcat[...], preferred_element_type=f32)
+    lax.fori_loop(edge // 16, (TALL - edge) // 16, activate, 0)
+
+    for copy in halos:
+        copy.wait_recv()
+    learn(0)
+    hot = one_hot(near_codes[0, 7:8], near_codes[1, 0:1])
+    windows_t = windows_of(hot)
+    ends = jnp.concatenate(
+        [windows_t[:, 0:128].T[0:edge], windows_t[:, ROWS : ROWS + 128].T[0:edge]], axis=0
+    ).astype(bf16)
+    ends = jnp.dot(ends, wcat[...], preferred_element_type=f32)
+    stem[0:edge] = ends[0:edge]
+    stem[TALL - edge :] = ends[edge:]
+    for i in (0, 1, TALL // 16 - 2, TALL // 16 - 1):
+        activate(i, 0)
     inside_left = jnp.where(ctx > 0, 1.0, 0.0)
     inside_right = jnp.where(ctx < count - 1, 1.0, 0.0)
     gx[0:LEAD] = gx[0:LEAD] * inside_left
@@ -280,6 +290,9 @@
         d_pooled[rows] = dpool.astype(bf16)
         dstem[rows, 0:C] = (dpool * slopes[more, 0:C]).astype(bf16)
         dstem[rows, C:] = (dpool * slopes[more, C:]).astype(bf16)
+    wins_t[...] = jnp.concatenate(
+        [pltpu.roll(hot, LANES - (PAIRS + LEAD + q), 1)[:, :ROWS] for q in range(8)], axis=0
+    ).astype(bf16)
     grad = jnp.dot(wins_t[...], dstem[...], preferred_element_type=f32)
     for k in range(3):
         tsum[k * 64 : k * 64 + 64] = grad[:, 128 * k : 128 * (k + 1)]

time: 62.6 us -> 60.4 us (0.965)
  Pallas kernels: 61.8 us -> 59.6 us
    pallas_call x1, Pallas kernels: 59.2 us -> 57.1 us  [main(): pl.pallas_call(functools.partial(main_kernel, ring, deep, high, count), o...]
where the time goes in v6:
time: 60.4 us; the launch traced here: 60.3 us
  Pallas kernels  59.6 us (99%)
  between operations  0.64 us (1%)
    pallas_call x1, Pallas kernels, main(): pl.pallas_call(functools.partial(main_kernel, ring, deep, high, count), o...  57.1 us
    pallas_call x1, Pallas kernels, finish(): pl.pallas_call(finish_kernel, out_shape=(jax.ShapeDtypeStruct((5, C, C),...  2.59 us

profile of v6, /device:TPU:1, one launch (start us, length us, event | category | flops | bytes accessed | tf_op | source)
XLA Modules:
  0.0 60.3 jit_solution(15793980661272937125)
XLA Ops:
  0.6 57.1 %block.1 = (bf16[512,384]{1,0:T(8,128)(2,1)S(1)}, bf16[512,384]{1,0:T(8,128)(2,1)S(1)}, bf16[2,2,4,4,96,128]{5,4,3,2,1,0:T(8,128)(2,1)S(1)}, bf16[2,96,128]{2,1,0:T(8,128)(2,1)S(1)}) custom-call(s32[1,64]{1,0:T(1,128)} %vpos_in.1, s32[1,64]{1,0:T(1,128)} %vshift_in.1, s32[8,128]{1,0:T(8,128)} %bitcast.7, bf16[512,384]{1,0:T(8,128)(2,1)} %bitcast.6, ...), custom_call_target="tpu_custom_call" | custom-call | tf_op jit(solution)/shard_map/block/pallas_call | solution.py:490
  57.7 2.6 %finish.1 = (f32[5,384,384]{2,1,0:T(8,128)}, f32[15,4,384]{2,1,0:T(4,128)}, bf16[512,384]{1,0:T(8,128)(2,1)}, bf16[512,384]{1,0:T(8,128)(2,1)}) custom-call(bf16[16,384,128]{2,1,0:T(8,128)(2,1)S(1)} %bitcast.5, bf16[2,96,128]{2,1,0:T(8,128)(2,1)S(1)} %get-tuple-element.13.small, bf16[512,384]{1,0:T(8,128)(2,1)S(1)} %get-tuple-element.14.features, ...), custom_call_target="tpu_custom_call" | custom-call | tf_op jit(solution)/shard_map/finish/pallas_call | solution.py:587

commit v7 on v6

--- a/solution.py
+++ b/solution.py
@@ -51,16 +51,19 @@
     wt, wf, wsem, ws, stem, slopes, cotx, gx, pooled, pslope, shifted, spread, wins_t, gated_t, dstem,
     own, s0, r0, s1, r1, s2, r2,
     t0, u0, tsum, t1, u1, t2, u2,
-    v3, s3, r3, g3, w3, v4, s4, r4, g4, w4,
-    c0s, c0r, c1s, c1r, c2s, c2r, c3s, c3r, d3s, d3r, d2s, d2r, d1s, d1r, d0s, d0r,
-    e0s, e0r, e1s, e1r, e2s, e2r, h0s, h0r, c4s, c4r, d4s, d4r,
+    v3a, s3a, r3a, g3a, w3a, v3b, s3b, r3b, g3b, w3b, v4, s4, r4, g4, w4,
+    c0s, c0r, c1s, c1r, c2s, c2r, c3sa, c3ra, d3sa, d3ra, d2s, d2r, d1s, d1r, d0s, d0r,
+    e0s, e0r, e1s, e1r, e2s, e2r, h0s, h0r, c4s, c4r, d4s, d4r, c3sb, c3rb, d3sb, d3rb,
 ):
     x, y, z, core, device = places(ring, deep, high)
+    v3, s3, r3, g3, w3 = (v3a, v3b), (s3a, s3b), (r3a, r3b), (g3a, g3b), (w3a, w3b)
+    c3s, c3r, d3s, d3r = (c3sa, c3sb), (c3ra, c3rb), (d3sa, d3sb), (d3ra, d3rb)
     ctx = lax.axis_index("context")
     other = 1 - core
     per = 4 // ring
     rows1 = per * C
     rows2 = rows1 // ring
+    rows3 = rows2 // 2
 
     def along(half, level, step):
         if (half == 0) == (level == 1):
@@ -242,7 +245,7 @@
         for k in range(2):
             half, sub = divmod(2 * j + k, 4)
             piece, sub = divmod(sub, per)
-            some = block[:, 128 * k : 128 * (k + 1)].reshape(parts, rows2, 128)
+            some = block[:, 128 * k : 128 * (k + 1)].reshape(parts, 2, rows3, 128)
             s0[half, piece, sub * parts : (sub + 1) * parts] = some.astype(bf16)
             if sub == per - 1:
                 level0(half, piece).start()
@@ -251,7 +254,7 @@
         for k in range(2):
             half, sub = divmod(2 * j + k, 4)
             piece, sub = divmod(sub, per)
-            some = block[:, 128 * k : 128 * (k + 1)].reshape(parts, rows2, 128)
+            some = block[:, 128 * k : 128 * (k + 1)].reshape(parts, 2, rows3, 128)
             own[half, piece, sub * parts : (sub + 1) * parts] = some
 
     def ahead(half, level, step):
@@ -260,21 +263,22 @@
     def behind(half, level, step):
         return lax.rem(mine(half, level) + ring - step, ring)
 
-    def level1(half, step, chunk):
+    def level1(half, step, chunk, q):
         return remote(
-            s1.at[half, step - 1, chunk], r1.at[half, step - 1, chunk],
-            c1s.at[half, step - 1, chunk], c1r.at[half, step - 1, chunk], along(half, 1, step),
+            s1.at[half, step - 1, chunk, q], r1.at[half, step - 1, chunk, q],
+            c1s.at[half, step - 1, chunk, q], c1r.at[half, step - 1, chunk, q], along(half, 1, step),
         )
 
     for half in range(2):
         for piece in range(ring):
             level0(half, piece).wait_recv()
-    for chunk in order + [0]:
-        for step in order:
-            for half in range(2):
-                at = ahead(half, 1, step), ahead(half, 2, chunk)
-                s1[half, step - 1, chunk] = (own[half, at[0], at[1]] + r0[half, at[0], at[1]].astype(f32)).astype(bf16)
-                level1(half, step, chunk).start()
+    for q in range(2):
+        for chunk in order + [0]:
+            for step in order:
+                for half in range(2):
+                    at = ahead(half, 1, step), ahead(half, 2, chunk), q
+                    s1[half, step - 1, chunk, q] = (own[(half, *at)] + r0[(half, *at)].astype(f32)).astype(bf16)
+                    level1(half, step, chunk, q).start()
 
     learn(1)
     for load in loads:
@@ -325,31 +329,25 @@
     for step in order:
         stem1(step).start()
 
-    def level2(half, step):
+    def level2(half, step, q):
         return remote(
-            s2.at[half, step - 1], r2.at[half, step - 1], c2s.at[half, step - 1], c2r.at[half, step - 1],
+            s2.at[half, step - 1, q], r2.at[half, step - 1, q], c2s.at[half, step - 1, q], c2r.at[half, step - 1, q],
             along(half, 2, step),
         )
 
-    for chunk in order + [0]:
-        for half in range(2):
-            at = mine(half, 1), ahead(half, 2, chunk)
-            total = own[half, at[0], at[1]] + r0[half, at[0], at[1]].astype(f32)
-            for step in range(1, ring):
-                level1(half, step, chunk).wait_recv()
-                total = total + r1[half, step - 1, chunk].astype(f32)
-            if chunk:
-                s2[half, chunk - 1] = total.astype(bf16)
-                level2(half, chunk).start()
-            else:
-                v3[half * rows2 : (half + 1) * rows2] = total
-
-    for step in range(1, ring):
-        stem1(step).wait_recv()
-        small = small + u1[step - 1].astype(f32)
-    t2[...] = small.astype(bf16)
-    for step in order:
-        stem2(step).start()
+    def second(q):
+        for chunk in order + [0]:
+            for half in range(2):
+                at = mine(half, 1), ahead(half, 2, chunk), q
+                total = own[(half, *at)] + r0[(half, *at)].astype(f32)
+                for step in range(1, ring):
+                    level1(half, step, chunk, q).wait_recv()
+                    total = total + r1[half, step - 1, chunk, q].astype(f32)
+                if chunk:
+                    s2[half, chunk - 1, q] = total.astype(bf16)
+                    level2(half, chunk, q).start()
+                else:
+                    v3[q][half * rows3 : (half + 1) * rows3] = total
 
     def far(i):
         half_way = deep // 2 - lax.div(i + 1, 2)
@@ -393,54 +391,73 @@
 
         return lax.fori_loop(0, deep - 1, one, send[z].astype(f32)).astype(bf16)
 
-    for half in range(2):
-        total = v3[half * rows2 : (half + 1) * rows2]
-        for step in near:
-            level2(half, step).wait_recv()
-            total = total + r2[half, step - 1].astype(f32)
-        v3[half * rows2 : (half + 1) * rows2] = total
-    conv_down, conv_up = down(s3, r3, c3s, c3r), up(g3, d3s, d3r)
+    share3 = 2 * rows3 // deep
+    conv_down = [down(s3[q], r3[q], c3s[q], c3r[q]) for q in range(2)]
+    conv_up = [up(g3[q], d3s[q], d3r[q]) for q in range(2)]
     stem_down, stem_up = down(s4, r4, c4s, c4r), up(g4, d4s, d4r)
-    for m in range(2, len(reach)):
-        learn(m)
-    cut(v3, s3, 2 * rows2 // deep)
-    start_all(conv_down)
+
+    for q in range(2):
+        second(q)
+        if q == 0:
+            for m in range(2, len(reach)):
+                learn(m)
+        else:
+            for step in range(1, ring):
+                stem1(step).wait_recv()
+                small = small + u1[step - 1].astype(f32)
+            t2[...] = small.astype(bf16)
+            for step in order:
+                stem2(step).start()
+        for half in range(2):
+            total = v3[q][half * rows3 : (half + 1) * rows3]
+            for step in near:
+                level2(half, step, q).wait_recv()
+                total = total + r2[half, step - 1, q].astype(f32)
+            v3[q][half * rows3 : (half + 1) * rows3] = total
+        cut(v3[q], s3[q], share3)
+        start_all(conv_down[q])
     for step in range(1, ring):
         stem2(step).wait_recv()
         small = small + u2[step - 1].astype(f32)
     v4[0:96] = small
     cut(v4, s4, 96 // deep)
     start_all(stem_down)
-    g3[z] = summed(conv_down, s3, r3)
-    start_all(conv_up)
+    for q in range(2):
+        g3[q][z] = summed(conv_down[q], s3[q], r3[q])
+        start_all(conv_up[q])
     g4[z] = summed(stem_down, s4, r4)
     start_all(stem_up)
-    each("wait_recv", conv_up)
-    join(g3, w3, 2 * rows2 // deep)
-
-    def back2(half, step):
-        spot = gathered.at[core, half, mine(half, 1), mine(half, 2)]
-        return remote(spot, spot, d2s.at[half, step - 1], d2r.at[half, step - 1], along(half, 2, step))
-
-    def back1(half, step, chunk):
-        spot = gathered.at[core, half, mine(half, 1), behind(half, 2, chunk)]
-        return remote(spot, spot, d1s.at[half, step - 1, chunk], d1r.at[half, step - 1, chunk], along(half, 1, step))
-
-    def back0(half, step, chunk):
-        spot = gathered.at[core, half, behind(half, 1, step), behind(half, 2, chunk)]
-        return remote(spot, spot, d0s.at[half, step, chunk], d0r.at[half, step, chunk], sibling)
-
-    for half in range(2):
-        gathered[core, half, mine(half, 1), mine(half, 2)] = w3[half * rows2 : (half + 1) * rows2].astype(bf16)
-        for step in order:
-            back2(half, step).start()
-    for chunk in [0] + near:
+
+    def back2(half, step, q):
+        spot = gathered.at[core, half, mine(half, 1), mine(half, 2), q]
+        return remote(spot, spot, d2s.at[half, step - 1, q], d2r.at[half, step - 1, q], along(half, 2, step))
+
+    def back1(half, step, chunk, q):
+        spot = gathered.at[core, half, mine(half, 1), behind(half, 2, chunk), q]
+        return remote(
+            spot, spot, d1s.at[half, step - 1, chunk, q], d1r.at[half, step - 1, chunk, q], along(half, 1, step)
+        )
+
+    def back0(half, step, chunk, q):
+        spot = gathered.at[core, half, behind(half, 1, step), behind(half, 2, chunk), q]
+        return remote(spot, spot, d0s.at[half, step, chunk, q], d0r.at[half, step, chunk, q], sibling)
+
+    for q in range(2):
+        each("wait_recv", conv_up[q])
+        join(g3[q], w3[q], share3)
         for half in range(2):
-            if chunk:
-                back2(half, chunk).wait_recv()
+            gathered[core, half, mine(half, 1), mine(half, 2), q] = w3[q][
+                half * rows3 : (half + 1) * rows3
+            ].astype(bf16)
             for step in order:
-                back1(half, step, chunk).start()
-            back0(half, 0, chunk).start()
+                back2(half, step, q).start()
+        for chunk in [0] + near:
+            for half in range(2):
+                if chunk:
+                    back2(half, chunk, q).wait_recv()
+                for step in order:
+                    back1(half, step, chunk, q).start()
+                back0(half, 0, chunk, q).start()
 
     each("wait_recv", stem_up)
     join(g4, w4, 96 // deep)
@@ -450,11 +467,12 @@
 
     stem_all[core] = w4[0:96].astype(bf16)
     back_stem().start()
-    for chunk in [0] + near:
-        for step in near:
-            for half in range(2):
-                back1(half, step, chunk).wait_recv()
-                back0(half, step, chunk).start()
+    for q in range(2):
+        for chunk in [0] + near:
+            for step in near:
+                for half in range(2):
+                    back1(half, step, chunk, q).wait_recv()
+                    back0(half, step, chunk, q).start()
     back_stem().wait()
     for copy in halos:
         copy.wait_send()
@@ -463,24 +481,28 @@
         for step in range(ring):
             level0(half, step).wait_send()
             for chunk in range(ring):
-                back0(half, step, chunk).wait()
+                for q in range(2):
+                    back0(half, step, chunk, q).wait()
         for step in range(1, ring):
-            level2(half, step).wait_send()
-            back2(half, step).wait_send()
-            for chunk in range(ring):
-                level1(half, step, chunk).wait_send()
-                back1(half, step, chunk).wait_send()
+            for q in range(2):
+                level2(half, step, q).wait_send()
+                back2(half, step, q).wait_send()
+                for chunk in range(ring):
+                    level1(half, step, chunk, q).wait_send()
+                    back1(half, step, chunk, q).wait_send()
     for step in range(1, ring):
         stem1(step).wait_send()
         stem2(step).wait_send()
-    each("wait_send", conv_down, conv_up, stem_down, stem_up)
+    each("wait_send", *conv_down, *conv_up, stem_down, stem_up)
 
 
 def main(ring, deep, high, vpos, vshift, codes, cot, stem_weight, weight):
     per = 4 // ring
     rows1 = per * C
     rows2 = rows1 // ring
-    talls = [-(-total // (8 * deep)) * 8 for total in (2 * rows2, 96)]
+    rows3 = rows2 // 2
+    totals = (2 * rows3, 2 * rows3, 96)
+    talls = [-(-total // (8 * deep)) * 8 for total in totals]
     count = 2 * (ring // high) * deep
     dma = pltpu.SemaphoreType.DMA
     halves = lambda *lead: pltpu.VMEM((2,) + lead, bf16)
@@ -492,7 +514,7 @@
         out_shape=(
             jax.ShapeDtypeStruct((ROWS, C), bf16),
             jax.ShapeDtypeStruct((ROWS, C), bf16),
-            jax.ShapeDtypeStruct((2, 2, ring, ring, rows2, 128), bf16),
+            jax.ShapeDtypeStruct((2, 2, ring, ring, 2, rows3, 128), bf16),
             jax.ShapeDtypeStruct((2, 96, 128), bf16),
         ),
         in_specs=[hbm] * 6,
@@ -524,13 +546,13 @@
             pltpu.VMEM((64, ROWS), bf16),
             pltpu.VMEM((C, ROWS), bf16),
             pltpu.VMEM((ROWS, 2 * C), bf16),
-            pltpu.VMEM((2, ring, ring, rows2, 128), f32),
-            halves(ring, ring, rows2, 128),
-            halves(ring, ring, rows2, 128),
-            halves(ring - 1, ring, rows2, 128),
-            halves(ring - 1, ring, rows2, 128),
-            halves(ring - 1, rows2, 128),
-            halves(ring - 1, rows2, 128),
+            pltpu.VMEM((2, ring, ring, 2, rows3, 128), f32),
+            halves(ring, ring, 2, rows3, 128),
+            halves(ring, ring, 2, rows3, 128),
+            halves(ring - 1, ring, 2, rows3, 128),
+            halves(ring - 1, ring, 2, rows3, 128),
+            halves(ring - 1, 2, rows3, 128),
+            halves(ring - 1, 2, rows3, 128),
             pltpu.VMEM((96, 128), bf16),
             pltpu.VMEM((96, 128), bf16),
             pltpu.VMEM((192, 128), f32),
@@ -540,7 +562,7 @@
             pltpu.VMEM((ring - 1, 96, 128), bf16),
             *[
                 scratch
-                for tall, total in zip(talls, (2 * rows2, 96))
+                for tall, total in zip(talls, totals)
                 for scratch in (
                     pltpu.VMEM((total + tall, 128), f32),
                     pltpu.VMEM((deep, tall, 128), bf16),
@@ -549,10 +571,10 @@
                     pltpu.VMEM((total + tall, 128), f32),
                 )
             ],
-            *pair(2, ring), *pair(2, ring - 1, ring), *pair(2, ring - 1), *pair(deep - 1),
-            *pair(deep - 1), *pair(2, ring - 1), *pair(2, ring - 1, ring), *pair(2, ring, ring),
+            *pair(2, ring), *pair(2, ring - 1, ring, 2), *pair(2, ring - 1, 2), *pair(deep - 1),
+            *pair(deep - 1), *pair(2, ring - 1, 2), *pair(2, ring - 1, ring, 2), *pair(2, ring, ring, 2),
             *pair(), *pair(ring - 1), *pair(ring - 1), *pair(),
-            *pair(deep - 1), *pair(deep - 1),
+            *pair(deep - 1), *pair(deep - 1), *pair(deep - 1), *pair(deep - 1),
         ],
         compiler_params=pltpu.CompilerParams(
             collective_id=0, has_side_effects=True, vmem_limit_bytes=36 * 1024 * 1024

time: 60.4 us -> 65 us (1.076)
  Pallas kernels: 59.6 us -> 64.2 us
    pallas_call x1, Pallas kernels: 57.1 us -> 61.6 us  [main(): pl.pallas_call(functools.partial(main_kernel, ring, deep, high, count), o...]
where the time goes in v7:
time: 65 us; the launch traced here: 64.9 us
  Pallas kernels  64.2 us (99%)
    pallas_call x1, Pallas kernels, main(): pl.pallas_call(functools.partial(main_kernel, ring, deep, high, count), o...  61.6 us
    pallas_call x1, Pallas kernels, finish(): pl.pallas_call(finish_kernel, out_shape=(jax.ShapeDtypeStruct((5, C, C),...  2.59 us

profile of v7, /device:TPU:1, one launch (start us, length us, event | category | flops | bytes accessed | tf_op | source)
XLA Modules:
  0.0 64.9 jit_solution(10215507804246910738)
XLA Ops:
  0.6 61.6 %block.1 = (bf16[512,384]{1,0:T(8,128)(2,1)S(1)}, bf16[512,384]{1,0:T(8,128)(2,1)S(1)}, bf16[2,2,4,4,2,48,128]{6,5,4,3,2,1,0:T(8,128)(2,1)S(1)}, bf16[2,96,128]{2,1,0:T(8,128)(2,1)S(1)}) custom-call(s32[1,64]{1,0:T(1,128)} %vpos_in.1, s32[1,64]{1,0:T(1,128)} %vshift_in.1, s32[8,128]{1,0:T(8,128)} %bitcast.7, bf16[512,384]{1,0:T(8,128)(2,1)} %bitcast.6, ...), custom_call_target="tpu_custom_call" | custom-call | tf_op jit(solution)/shard_map/block/pallas_call | solution.py:512
  62.3 2.6 %finish.1 = (f32[5,384,384]{2,1,0:T(8,128)}, f32[15,4,384]{2,1,0:T(4,128)}, bf16[512,384]{1,0:T(8,128)(2,1)}, bf16[512,384]{1,0:T(8,128)(2,1)}) custom-call(bf16[16,384,128]{2,1,0:T(8,128)(2,1)S(1)} %bitcast.5, bf16[2,96,128]{2,1,0:T(8,128)(2,1)S(1)} %get-tuple-element.13.small, bf16[512,384]{1,0:T(8,128)(2,1)S(1)} %get-tuple-element.14.features, ...), custom_call_target="tpu_custom_call" | custom-call | tf_op jit(solution)/shard_map/finish/pallas_call | solution.py:609

commit v8 on v6

--- a/solution.py
+++ b/solution.py
@@ -388,8 +388,9 @@
 
     def summed(copy, send, land):
         def one(i, total):
-            copy(i + 1).wait_recv()
-            return total + land[i].astype(f32)
+            step = far(deep - 2 - i)
+            copy(step).wait_recv()
+            return total + land[step - 1].astype(f32)
 
         return lax.fori_loop(0, deep - 1, one, send[z].astype(f32)).astype(bf16)
 
@@ -411,10 +412,24 @@
     v4[0:96] = small
     cut(v4, s4, 96 // deep)
     start_all(stem_down)
+    for half in range(2):
+        for step in range(ring):
+            level0(half, step).wait_send()
+        for step in range(1, ring):
+            level2(half, step).wait_send()
+            for chunk in range(ring):
+                level1(half, step, chunk).wait_send()
+    stem0().wait_send()
+    for step in range(1, ring):
+        stem1(step).wait_send()
+        stem2(step).wait_send()
+    for copy in halos:
+        copy.wait_send()
     g3[z] = summed(conv_down, s3, r3)
     start_all(conv_up)
     g4[z] = summed(stem_down, s4, r4)
     start_all(stem_up)
+    each("wait_send", conv_down, stem_down)
     each("wait_recv", conv_up)
     join(g3, w3, 2 * rows2 // deep)
 
@@ -450,30 +465,26 @@
 
     stem_all[core] = w4[0:96].astype(bf16)
     back_stem().start()
+    each("wait_send", conv_up, stem_up)
+    last = []
     for chunk in [0] + near:
+        fresh = [(half, 0, chunk) for half in range(2)]
         for step in near:
             for half in range(2):
                 back1(half, step, chunk).wait_recv()
                 back0(half, step, chunk).start()
-    back_stem().wait()
-    for copy in halos:
-        copy.wait_send()
-    stem0().wait_send()
+                fresh.append((half, step, chunk))
+        for spot in last:
+            back0(*spot).wait()
+        last = fresh
     for half in range(2):
-        for step in range(ring):
-            level0(half, step).wait_send()
-            for chunk in range(ring):
-                back0(half, step, chunk).wait()
         for step in range(1, ring):
-            level2(half, step).wait_send()
             back2(half, step).wait_send()
             for chunk in range(ring):
-                level1(half, step, chunk).wait_send()
                 back1(half, step, chunk).wait_send()
-    for step in range(1, ring):
-        stem1(step).wait_send()
-        stem2(step).wait_send()
-    each("wait_send", conv_down, conv_up, stem_down, stem_up)
+    back_stem().wait()
+    for spot in last:
+        back0(*spot).wait()
 
 
 def main(ring, deep, high, vpos, vshift, codes, cot, stem_weight, weight):

time: 60.4 us -> 60.4 us (level)
  no operation moved by 1% of the time
where the time goes in v8:
time: 60.4 us; the launch traced here: 60.3 us
  Pallas kernels  59.7 us (99%)
  between operations  0.64 us (1%)
    pallas_call x1, Pallas kernels, main(): pl.pallas_call(functools.partial(main_kernel, ring, deep, high, count), o...  57.1 us
    pallas_call x1, Pallas kernels, finish(): pl.pallas_call(finish_kernel, out_shape=(jax.ShapeDtypeStruct((5, C, C),...  2.59 us

profile of v8, /device:TPU:1, one launch (start us, length us, event | category | flops | bytes accessed | tf_op | source)
XLA Modules:
  0.0 60.3 jit_solution(5409125925496062637)
XLA Ops:
  0.6 57.1 %block.1 = (bf16[512,384]{1,0:T(8,128)(2,1)S(1)}, bf16[512,384]{1,0:T(8,128)(2,1)S(1)}, bf16[2,2,4,4,96,128]{5,4,3,2,1,0:T(8,128)(2,1)S(1)}, bf16[2,96,128]{2,1,0:T(8,128)(2,1)S(1)}) custom-call(s32[1,64]{1,0:T(1,128)} %vpos_in.1, s32[1,64]{1,0:T(1,128)} %vshift_in.1, s32[8,128]{1,0:T(8,128)} %bitcast.7, bf16[512,384]{1,0:T(8,128)(2,1)} %bitcast.6, ...), custom_call_target="tpu_custom_call" | custom-call | tf_op jit(solution)/shard_map/block/pallas_call | solution.py:501
  57.7 2.6 %finish.1 = (f32[5,384,384]{2,1,0:T(8,128)}, f32[15,4,384]{2,1,0:T(4,128)}, bf16[512,384]{1,0:T(8,128)(2,1)}, bf16[512,384]{1,0:T(8,128)(2,1)}) custom-call(bf16[16,384,128]{2,1,0:T(8,128)(2,1)S(1)} %bitcast.5, bf16[2,96,128]{2,1,0:T(8,128)(2,1)S(1)} %get-tuple-element.13.small, bf16[512,384]{1,0:T(8,128)(2,1)S(1)} %get-tuple-element.14.features, ...), custom_call_target="tpu_custom_call" | custom-call | tf_op jit(solution)/shard_map/finish/pallas_call | solution.py:598

commit v9 on v8

--- a/solution.py
+++ b/solution.py
@@ -260,21 +260,24 @@
     def behind(half, level, step):
         return lax.rem(mine(half, level) + ring - step, ring)
 
-    def level1(half, step, chunk):
+    sequence = order + [0]
+
+    def level1(half, step, group):
         return remote(
-            s1.at[half, step - 1, chunk], r1.at[half, step - 1, chunk],
-            c1s.at[half, step - 1, chunk], c1r.at[half, step - 1, chunk], along(half, 1, step),
+            s1.at[half, step - 1, 2 * group : 2 * group + 2], r1.at[half, step - 1, 2 * group : 2 * group + 2],
+            c1s.at[half, step - 1, group], c1r.at[half, step - 1, group], along(half, 1, step),
         )
 
     for half in range(2):
         for piece in range(ring):
             level0(half, piece).wait_recv()
-    for chunk in order + [0]:
+    for slot, chunk in enumerate(sequence):
         for step in order:
             for half in range(2):
                 at = ahead(half, 1, step), ahead(half, 2, chunk)
-                s1[half, step - 1, chunk] = (own[half, at[0], at[1]] + r0[half, at[0], at[1]].astype(f32)).astype(bf16)
-                level1(half, step, chunk).start()
+                s1[half, step - 1, slot] = (own[half, at[0], at[1]] + r0[half, at[0], at[1]].astype(f32)).astype(bf16)
+                if slot % 2:
+                    level1(half, step, slot // 2).start()
 
     learn(1)
     for load in loads:
@@ -331,13 +334,14 @@
             along(half, 2, step),
         )
 
-    for chunk in order + [0]:
+    for slot, chunk in enumerate(sequence):
         for half in range(2):
             at = mine(half, 1), ahead(half, 2, chunk)
             total = own[half, at[0], at[1]] + r0[half, at[0], at[1]].astype(f32)
             for step in range(1, ring):
-                level1(half, step, chunk).wait_recv()
-                total = total + r1[half, step - 1, chunk].astype(f32)
+                if slot % 2 == 0:
+                    level1(half, step, slot // 2).wait_recv()
+                total = total + r1[half, step - 1, slot].astype(f32)
             if chunk:
                 s2[half, chunk - 1] = total.astype(bf16)
                 level2(half, chunk).start()
@@ -417,8 +421,8 @@
             level0(half, step).wait_send()
         for step in range(1, ring):
             level2(half, step).wait_send()
-            for chunk in range(ring):
-                level1(half, step, chunk).wait_send()
+            for group in range(ring // 2):
+                level1(half, step, group).wait_send()
     stem0().wait_send()
     for step in range(1, ring):
         stem1(step).wait_send()

time: 60.4 us -> 61.2 us (1.013)
  Pallas kernels: 59.7 us -> 60.4 us
    pallas_call x1, Pallas kernels: 57.1 us -> 57.8 us  [main(): pl.pallas_call(functools.partial(main_kernel, ring, deep, high, count), o...]
where the time goes in v9:
time: 61.2 us; the launch traced here: 61.1 us
  Pallas kernels  60.4 us (99%)
  between operations  0.64 us (1%)
    pallas_call x1, Pallas kernels, main(): pl.pallas_call(functools.partial(main_kernel, ring, deep, high, count), o...  57.8 us
    pallas_call x1, Pallas kernels, finish(): pl.pallas_call(finish_kernel, out_shape=(jax.ShapeDtypeStruct((5, C, C),...  2.59 us

profile of v9, /device:TPU:1, one launch (start us, length us, event | category | flops | bytes accessed | tf_op | source)
XLA Modules:
  0.0 61.1 jit_solution(10945827335610626527)
XLA Ops:
  0.6 57.8 %block.1 = (bf16[512,384]{1,0:T(8,128)(2,1)S(1)}, bf16[512,384]{1,0:T(8,128)(2,1)S(1)}, bf16[2,2,4,4,96,128]{5,4,3,2,1,0:T(8,128)(2,1)S(1)}, bf16[2,96,128]{2,1,0:T(8,128)(2,1)S(1)}) custom-call(s32[1,64]{1,0:T(1,128)} %vpos_in.1, s32[1,64]{1,0:T(1,128)} %vshift_in.1, s32[8,128]{1,0:T(8,128)} %bitcast.7, bf16[512,384]{1,0:T(8,128)(2,1)} %bitcast.6, ...), custom_call_target="tpu_custom_call" | custom-call | tf_op jit(solution)/shard_map/block/pallas_call | solution.py:505
  58.5 2.6 %finish.1 = (f32[5,384,384]{2,1,0:T(8,128)}, f32[15,4,384]{2,1,0:T(4,128)}, bf16[512,384]{1,0:T(8,128)(2,1)}, bf16[512,384]{1,0:T(8,128)(2,1)}) custom-call(bf16[16,384,128]{2,1,0:T(8,128)(2,1)S(1)} %bitcast.5, bf16[2,96,128]{2,1,0:T(8,128)(2,1)S(1)} %get-tuple-element.13.small, bf16[512,384]{1,0:T(8,128)(2,1)S(1)} %get-tuple-element.14.features, ...), custom_call_target="tpu_custom_call" | custom-call | tf_op jit(solution)/shard_map/finish/pallas_call | solution.py:602
